TPU v7x, 32 devices: a whole 2x2x4 slice. The times are simulated.
32 devices in a mesh: member: 2 (over x), lat: 16 (over z, y, core).
Axes of the slice: x: 2, y: 2, z: 4, core: 2. Of those that a mesh axis runs over, the one named last changes fastest.
Arguments:
- state: float32 [10, 128, 128, 256], P('member', None, 'lat'), parts along dimension 0, may hold values from -6 to 6
- wind: float32 [256, 128, 256], P('member', 'lat'), parts along dimension 0, may hold values from -0.9 to 0.9
- sunlight: float32 [256, 256], P(('member', 'lat')), parts along dimension 0, may hold values from 0.1 to 1
- day_list: int32 [32, 16], P(('member', 'lat')), parts along dimension 0, may hold values from -1 to 15, as said below
- w_first: bfloat16 [640, 2048], replicated, may hold values from -0.25 to 0.25
- bias: float32 [2048], replicated, may hold values from -3 to 3
- w_second: bfloat16 [2048, 128], replicated, may hold values from -0.125 to 0.125
- remap: float32 [128, 128], replicated, may hold values from -1.5 to 2
Outputs:
- new_state: float32 [10, 128, 128, 256], P('member', None, 'lat'), parts along dimension 0
There are 2 independent parts, one for each index of `member`. A program takes and returns all parts, laid end to end along the dimension named above; an argument that names none is the same for every part. Nothing has to cross between parts.
Inputs may be any that keep to these rules, and one draw needn't show every extreme that they name: `day_list`: row d names the daylit blocks of band d, each once, as a cyclic run of consecutive numbers placed first, then -1; every row names at least one block. Rows d and d + 8 together name at most 20 blocks; row 0 names all 16 and row 8 exactly 4.
All inputs are finite; a program needn't handle non-finite values.
Results may differ from a plain program's by a relative error of at most 0.00062.
Values may be sent and summed in bfloat16 or wider, within the bound.
No kernel may reach another device: no remote copies, remote signals or barrier semaphores. Data moves between devices by JAX's collectives and lax.ppermute only.
A program may use at most 128 MiB of HBM per device.

v0:
```python
import functools
import jax
import jax.numpy as jnp
from jax import lax
from jax.experimental import pallas as pl
from jax.experimental.pallas import tpu as pltpu
from jax.sharding import PartitionSpec as P

LANES = 128
CODE = 80.0
GELU_A = 0.7978845608028654
GELU_B = 0.7978845608028654 * 0.044715
HBM = pl.BlockSpec(memory_space=pltpu.HBM)
VMEM = pl.BlockSpec(memory_space=pltpu.VMEM)
MIB = 1024 * 1024


def call(kernel, outs, operands, ins=None, out_specs=None, scratch=(), limit=8, flops=0, moved=0, alias=None):
    return pl.pallas_call(
        kernel,
        in_specs=ins or [VMEM] * len(operands),
        out_specs=out_specs or [VMEM] * len(outs),
        out_shape=outs,
        scratch_shapes=scratch,
        input_output_aliases=alias or {},
        compiler_params=pltpu.CompilerParams(vmem_limit_bytes=limit * MIB),
        cost_estimate=pl.CostEstimate(flops=flops, bytes_accessed=moved, transcendentals=0),
    )(*operands)


def array(shape, dtype=jnp.float32):
    return jax.ShapeDtypeStruct(shape, dtype)


def limited(ahead, behind):
    return jnp.maximum(jnp.minimum(ahead, jnp.maximum(behind, 0.0)), jnp.minimum(behind, 0.0))


def face(speed):
    size = jnp.abs(speed)
    return speed > 0.0, speed, size * (0.5 - 0.5 * size)


def rows_after(q, faces):
    diffs = [b - a for a, b in zip(q[:-1], q[1:])]
    slopes = [None] + [limited(b, a) for a, b in zip(diffs[:-1], diffs[1:])]
    fluxes = []
    for j, (mask, speed, half) in enumerate(faces):
        edge = jnp.where(mask, q[j + 1], q[j + 2])
        slope = jnp.where(mask, slopes[j + 1], slopes[j + 2])
        fluxes.append(speed * edge + half * slope)
    return [q[j + 2] - (fluxes[j + 1] - fluxes[j]) for j in range(len(faces) - 1)]


def encode(speed):
    size = jnp.exp(CODE * jnp.abs(speed))
    return jnp.where(speed < 0.0, -size, size).astype(jnp.bfloat16)


def decode(code):
    size = jnp.log(jnp.maximum(jnp.abs(code), 1.0)) * (1.0 / CODE)
    return jnp.where(code < 0.0, -size, size)


def is_even():
    return lax.rem(lax.axis_index("lat"), 2) == 0


def either(body, when_even):
    even = is_even()
    pl.when(even)(lambda: body(when_even))
    pl.when(jnp.logical_not(even))(lambda: body(not when_even))


def row_of(ref, start, count, rows):
    return ref[pl.ds(start, count, stride=rows), :]


def pack_kernel(half, parts, state_hbm, wind_hbm, kept_ref, winds_ref, near_ref, far_ref, sems):
    fields, levels, rows, lanes = kept_ref.shape
    size = levels // parts
    lon = pl.ds(half * lanes, lanes)
    copies = []
    for p in range(parts):
        some = pl.ds(p * size, size)
        made = pltpu.make_async_copy(state_hbm.at[:, some, :, lon], kept_ref.at[:, some], sems.at[p])
        made.start()
        copies.append(made)
    winds = pltpu.make_async_copy(wind_hbm.at[:, :, lon], winds_ref, sems.at[parts])
    winds.start()
    flat = kept_ref.reshape(fields * levels * rows, lanes)
    even = is_even()
    for p, made in enumerate(copies):
        made.wait()
        here = slice(p * size, (p + 1) * size)
        for f in range(fields):
            base = (f * levels + p * size) * rows
            for r in range(2):
                for ref, start in ((near_ref, jnp.where(even, rows - 2, 0)), (far_ref, jnp.where(even, 0, rows - 2))):
                    value = row_of(flat, base + start + r, size, rows)
                    ref[r * fields + f, here] = value.astype(jnp.bfloat16)
    winds.wait()
    speed = row_of(winds_ref.reshape(levels * rows, lanes), 0, levels, rows)
    code = encode(speed)
    for ref in (near_ref, far_ref):
        ref[2 * fields] = code


def pack(half, state, wind):
    fields, levels, rows, _ = state.shape
    parts = 4
    return call(
        functools.partial(pack_kernel, half, parts),
        [
            array((fields, levels, rows, LANES)),
            array((levels, rows, LANES)),
            array((2 * fields + 1, levels, LANES), jnp.bfloat16),
            array((2 * fields + 1, levels, LANES), jnp.bfloat16),
        ],
        (state, wind), ins=[HBM, HBM], scratch=[pltpu.SemaphoreType.DMA((parts + 1,))], moved=5_000_000)


def inner_kernel(kept_ref, winds_ref, out_ref):
    fields, levels, rows, lanes = kept_ref.shape
    step = 8
    flat = kept_ref.reshape(fields * levels * rows, lanes)
    winds = winds_ref.reshape(levels * rows, lanes)

    @pl.loop(0, levels // step)
    def _(i):
        base = i * (step * rows)
        faces = [face(row_of(winds, base + r, step, rows)) for r in range(2, rows - 1)]
        level = pl.multiple_of(i * step, step)
        for f in range(fields):
            q = [row_of(flat, f * levels * rows + base + r, step, rows) for r in range(rows)]
            for r, value in enumerate(rows_after(q, faces)):
                out_ref[r, f, pl.ds(level, step), :] = value


def inner(kept, winds):
    fields, levels, rows, lanes = kept.shape
    return call(
        inner_kernel, [array((rows - 4, fields, levels, lanes))], (kept, winds),
        flops=1_000_000, moved=1_000_000)[0]


def edge_kernel(near, kept_ref, winds_ref, halo_ref, out_ref, sent_ref):
    fields, levels, rows, lanes = kept_ref.shape
    step = 16
    flat = kept_ref.reshape(fields * levels * rows, lanes)
    winds = winds_ref.reshape(levels * rows, lanes)

    def body(bottom):
        first = rows - 2 if bottom else 0

        @pl.loop(0, levels // step)
        def _(i):
            base = i * (step * rows)
            here = pl.ds(pl.multiple_of(i * step, step), step)
            wide = lambda index: halo_ref[index, here, :].astype(jnp.float32)
            faces = [
                face(decode(wide(2 * fields)) if r == rows else row_of(winds, base + r, step, rows))
                for r in range(first, first + 3)
            ]
            for f in range(fields):
                own = lambda r: row_of(flat, f * levels * rows + base + r, step, rows)
                halo = [wide(f), wide(fields + f)]
                q = [own(r) for r in range(rows - 4, rows)] + halo if bottom else halo + [own(r) for r in range(4)]
                for r, value in enumerate(rows_after(q, faces)):
                    out_ref[r, f, here, :] = value
                    sent_ref[r * fields + f, here, :] = value.astype(jnp.bfloat16)

    either(body, near)


def edge(near, kept, winds, halo):
    fields, levels, _, lanes = kept.shape
    return call(
        functools.partial(edge_kernel, near),
        [array((2, fields, levels, lanes)), array((2 * fields, levels, lanes), jnp.bfloat16)],
        (kept, winds, halo), flops=1_000_000, moved=300_000)


def weights_kernel(first_ref, bias_ref, second_ref, remap_ref, first_out, second_out, split_out):
    inputs, hidden = first_ref.shape
    levels = remap_ref.shape[0]
    whole = remap_ref[...]
    r_high = whole.astype(jnp.bfloat16)
    r_low = (whole - r_high.astype(jnp.float32)).astype(jnp.bfloat16)
    for j in range(2):
        split_out[:levels, j * levels : (j + 1) * levels] = r_high
        split_out[levels:, j * levels : (j + 1) * levels] = r_low
    chunk = 256
    same = lambda d: lax.broadcasted_iota(jnp.int32, (chunk, chunk), d)
    unit = jnp.where(same(0) == same(1), 1.0, 0.0).astype(jnp.bfloat16)
    flip = lambda part: lax.dot_general(
        unit, part, (((1,), (1,)), ((), ())), preferred_element_type=jnp.float32).astype(jnp.bfloat16)
    small = unit[:LANES, :LANES]
    row = lax.broadcasted_iota(jnp.int32, (LANES, chunk), 0)
    for j in range(hidden // chunk):
        here = slice(j * chunk, (j + 1) * chunk)
        first_out[here, :inputs] = flip(first_ref[:, here])
        bias = bias_ref[:, here]
        high = bias.astype(jnp.bfloat16).astype(jnp.float32)
        middle = (bias - high).astype(jnp.bfloat16).astype(jnp.float32)
        low = bias - high - middle
        stacked = jnp.where(row == 0, high, jnp.where(row == 1, middle, jnp.where(row == 2, low, 0.0)))
        first_out[here, inputs:] = flip(stacked.astype(jnp.bfloat16))
        second_out[:, here] = lax.dot_general(
            small, second_ref[here, :], (((1,), (1,)), ((), ())),
            preferred_element_type=jnp.float32).astype(jnp.bfloat16)


def weights(w_first, bias, w_second, remap):
    inputs, hidden = w_first.shape
    levels = remap.shape[0]
    outputs = w_second.shape[1]
    return call(
        weights_kernel,
        [
            array((hidden, inputs + LANES), jnp.bfloat16),
            array((outputs, hidden), jnp.bfloat16),
            array((2 * levels, 2 * levels), jnp.bfloat16),
        ],
        (w_first, bias.reshape(1, hidden), w_second, remap), flops=50_000_000, moved=7_000_000)


def network(x, w1_ref, w2_ref, g_ref):
    hidden = w1_ref.shape[0]
    chunk = 512
    for c in range(hidden // chunk):
        here = slice(c * chunk, (c + 1) * chunk)
        v = jnp.dot(w1_ref[here, :], x, preferred_element_type=jnp.float32)
        h = 0.5 * v
        t = jnp.tanh(v * (GELU_A + GELU_B * (v * v)))
        g_ref[here, :] = (h + h * t).astype(jnp.bfloat16)
    return jnp.dot(w2_ref[...], g_ref[...], preferred_element_type=jnp.float32)


def advance(stage, half_refs, a, units, fields, levels, rows, lanes):
    mid, rim, wnd = half_refs[:3]
    step = 16
    winds = wnd.reshape(levels * rows, lanes)
    near = stage == "near"

    def body(bottom):
        if stage == "near":
            first, many = (rows - 4 if bottom else 0), 4
        elif stage == "between":
            first, many = (rows - 4 if bottom else 2), 2
        else:
            first, many = (rows - 2 if bottom else 0), 2

        @pl.loop(0, levels // step)
        def _(i):
            here = pl.ds(pl.multiple_of(i * step, step), step)
            there = pl.ds(pl.multiple_of(levels + i * step, step), step)
            base = i * (step * rows)
            wide = lambda ref, index: ref[index, here, :].astype(jnp.float32)

            def value_of(r, f):
                if r < 0:
                    return wide(half_refs[3], (r + 2) * fields + f)
                if r >= rows:
                    return wide(half_refs[3], (r - rows) * fields + f)
                if 2 <= r < rows - 2:
                    return mid[r - 2, f, here, :]
                return rim[r - (rows - 2) if bottom else r, f, here, :]

            faces = [
                face(decode(wide(half_refs[4], 2 * fields)) if r == rows else row_of(winds, base + r, step, rows))
                for r in range(first, first + many + 1)
            ]
            for f in range(fields):
                q = [value_of(r, f) for r in range(first - 2, first + many + 2)]
                for j, value in enumerate(rows_after(q, faces)):
                    u, place = units[j // 2], j % 2
                    cols = pl.ds(place * lanes, lanes)
                    high = value.astype(jnp.bfloat16)
                    a[u, f, here, cols] = high
                    a[u, f, there, cols] = (value - high.astype(jnp.float32)).astype(jnp.bfloat16)

    either(body, near)


def finish_kernel(stage, group, halves, *refs):
    days, sun, rcat, w1, w2, *refs = refs
    n = len(group)
    per = {"near": 5, "between": 3, "far": 5}[stage]
    parts = [refs[k * per : (k + 1) * per] for k in range(n)]
    refs = refs[n * per :]
    if stage != "near":
        refs = refs[n:]
    far = stage == "far"
    ready = ()
    if far:
        ready, refs = refs[: group[0]], refs[group[0] :]
        out_hbm, *refs = refs[1:] if group[0] else refs
    outs, refs = refs[:n], refs[n:]
    a, x, rem, g, *sems = refs
    fields, levels, rows, lanes = outs[0].shape
    inputs = fields * levels
    stores = []

    def store(source, target):
        made = pltpu.make_async_copy(source, target, sems[0].at[len(stores)])
        made.start()
        stores.append(made)

    for h, source in enumerate(ready):
        store(source.at[0], out_hbm.at[0, :, :, pl.ds(h * lanes, lanes)])
    row = lax.broadcasted_iota(jnp.int32, (x.shape[1] - inputs, x.shape[2]), 0)
    for u in range(x.shape[0]):
        x[u, inputs:, :] = jnp.where(row < 3, 1.0, 0.0).astype(jnp.bfloat16)

    even = is_even()
    plan = []
    for k in range(n):
        advance(stage, parts[k], a, (0, 1) if stage == "near" else (k,), fields, levels, rows, lanes)
        if stage == "near":
            plan += [(0, k, (rows - 4, 0)), (1, k, (rows - 2, 2))]
        elif stage == "between":
            plan.append((k, k, (2, rows - 4)))
        else:
            plan.append((k, k, (0, rows - 2)))

    def put(f, k, start, place, value):
        flat = outs[k].reshape(fields * levels * rows, lanes)
        flat[pl.ds(f * levels * rows + start + place, levels, stride=rows), :] = value

    for u, k, starts in plan:
        start = jnp.where(even, *starts)
        for f in range(fields):
            both = jnp.dot(rcat[...], a[u, f], preferred_element_type=jnp.float32)
            value = both[:levels] + both[levels:]
            x[u, f * levels : (f + 1) * levels, :] = value.astype(jnp.bfloat16)
            if f == 0:
                rem[u] = value
            else:
                for place in range(2):
                    put(f, k, start, place, value[:, place * lanes : (place + 1) * lanes])
    lon = pl.ds(group[-1] * lanes, lanes)
    if far:
        most = pl.ds(1, fields - 1)
        store(outs[0].at[most], out_hbm.at[most, :, :, lon])
    for u, k, starts in plan:
        start = jnp.where(even, *starts)
        half = group[k]
        net = network(x[u], w1, w2, g.at[u])
        for place in range(2):
            block = (start + place) * halves + half
            lit = days[0, 0] == block
            for i in range(1, days.shape[1]):
                lit = jnp.logical_or(lit, days[0, i] == block)
            part = slice(place * lanes, (place + 1) * lanes)
            light = [sun[r + place : r + place + 1, half * lanes : (half + 1) * lanes] for r in starts]
            light = jnp.where(even, *light) * jnp.where(lit, 1.0, 0.0)
            put(0, k, start, place, rem[u, :, part] + net[:, part] * light)
    if far and group[0] == halves - 1:
        store(outs[0].at[0], out_hbm.at[0, :, :, lon])
    for made in stores:
        made.wait()


def finish(stage, group, halves, shared, parts, outs=(), ready=(), whole=()):
    _, _, _, w1, _ = shared
    levels, rows, lanes = parts[0][2].shape
    fields = parts[0][0].shape[1]
    units = 2 if stage == "near" else len(group)
    scratch = [
        pltpu.VMEM((units, fields, 2 * levels, 2 * lanes), jnp.bfloat16),
        pltpu.VMEM((units, w1.shape[1], 2 * lanes), jnp.bfloat16),
        pltpu.VMEM((units, levels, 2 * lanes), jnp.float32),
        pltpu.VMEM((units, w1.shape[0], 2 * lanes), jnp.bfloat16),
    ]
    operands = tuple(shared) + sum((tuple(p) for p in parts), ())
    alias = {len(operands) + k: k for k in range(len(outs))}
    operands += tuple(outs) + tuple(ready) + tuple(whole)
    results = [array((fields, levels, rows, lanes))] * len(group)
    out_specs = [VMEM] * len(group)
    ins = [pl.BlockSpec(memory_space=pltpu.SMEM)] + [VMEM] * (len(operands) - 1)
    if stage == "far":
        scratch.append(pltpu.SemaphoreType.DMA((halves + 1,)))
        results = [array((fields, levels, rows, halves * lanes))] + results
        out_specs = [HBM] + out_specs
        alias = {key: value + 1 for key, value in alias.items()}
        if whole:
            ins[-1] = HBM
            alias[len(operands) - 1] = 0
    return call(
        functools.partial(finish_kernel, stage, group, halves), results, operands,
        ins=ins, out_specs=out_specs,
        scratch=scratch, alias=alias, limit=16, flops=units * 1_000_000_000, moved=6_000_000)


def swap(block, route):
    return lax.ppermute(block, "lat", route)


def step_of(state, wind, sunlight, day_list, w_first, bias, w_second, remap):
    halves = state.shape[3] // LANES
    count = lax.axis_size("lat")
    near_route = [(i, i ^ 1) for i in range(count) if i ^ 1 < count]
    far_route = [(i, j) for i in range(count) for j in ((i - 1) if i % 2 == 0 else (i + 1),) if 0 <= j < count]
    every = range(halves)
    barrier = lax.optimization_barrier
    kept, winds, far, mid, near1, near2, rim = [], [], [], [], [], [], []
    for h in every:
        k, w, near_sent, far_sent = pack(
            h, pltpu.with_memory_space_constraint(state, pltpu.HBM), pltpu.with_memory_space_constraint(wind, pltpu.HBM))
        kept.append(k)
        winds.append(w)
        far.append(swap(far_sent, far_route))
        near = swap(near_sent, near_route)
        m = inner(k, w)
        m, near = barrier((m, near))
        mid.append(m)
        near1.append(near)
        rows, near_sent = edge(True, k, w, near)
        rim.append(rows)
        near2.append(swap(near_sent, near_route))
        if h + 1 < halves:
            wind, near_sent = barrier((wind, near_sent))
    w1, w2, rcat = weights(w_first, bias, w_second, remap)
    shared = (day_list, sunlight, rcat, w1, w2)
    far_rim, far2, outs = [], [], []
    for h in every:
        rows, far_sent = edge(False, kept[h], winds[h], far[h])
        far_rim.append(rows)
        far2.append(swap(far_sent, far_route))
        near2[h], far_sent = barrier((near2[h], far_sent))
        outs += finish("near", (h,), halves, shared, [(mid[h], rim[h], winds[h], near2[h], near1[h])])
        if h + 1 < halves:
            far[h + 1], outs[h] = barrier((far[h + 1], outs[h]))
    parts = [(mid[h], far_rim[h], winds[h]) for h in every]
    outs = list(finish("between", tuple(every), halves, shared, parts, outs))
    far2[0], outs = barrier((far2[0], outs))
    ready, whole = [], ()
    for h in every:
        part = parts[h] + (far2[h], far[h])
        result, done = finish("far", (h,), halves, shared, [part], [outs[h]], ready, whole)
        if h == halves - 1:
            return result
        ready.append(done)
        whole = (result,)
        far2[h + 1], ready, whole = barrier((far2[h + 1], ready, whole))


def solution(mesh):
    placed = (
        P("member", None, "lat", None),
        P("member", "lat", None),
        P(("member", "lat"), None),
        P(("member", "lat"), None),
        P(),
        P(),
        P(),
        P(),
    )
    return jax.shard_map(
        step_of,
        mesh=mesh,
        in_specs=placed,
        out_specs=P("member", None, "lat", None),
        check_vma=False,
    )
```

profile of v0, /device:TPU:1, one launch (start us, length us, event | category | flops | bytes accessed | tf_op | source)
XLA Modules:
  0.0 52.8 jit_solution(14724416454573957681)
XLA Ops:
  0.0 1.9 %shard_map.83 = (f32[5,128,8,128]{3,2,1,0:T(8,128)S(1)}, f32[128,8,128]{2,1,0:T(8,128)S(1)}, bf16[11,128,128]{2,1,0:T(8,128)(2,1)S(1)}, bf16[11,128,128]{2,1,0:T(8,128)(2,1)S(1)}) custom-call(f32[5,128,8,256]{3,2,1,0:T(8,128)} %state_hbm.3, f32[128,8,256]{2,1,0:T(8,128)} %wind_hbm.2), custom_call_target="tpu_custom_call" | custom-call | bytes 5000000 | tf_op jit(solution)/shard_map/pallas_call | solution.py:19
  2.0 0.1 collective-permute-start
  2.0 1.0 %shard_map.84.refs_5_ = f32[4,5,128,128]{3,2,1,0:T(8,128)S(1)} custom-call(f32[5,128,8,128]{3,2,1,0:T(8,128)S(1)} %get-tuple-element.47.kept_ref, f32[128,8,128]{2,1,0:T(8,128)S(1)} %get-tuple-element.48.winds_ref.refs_7_), custom_call_target="tpu_custom_call" | custom-call | flops 1000000 | bytes 1000000 | tf_op jit(solution)/shard_map/pallas_call | solution.py:19
  3.0 0.7 %collective-permute-done.halo_ref.refs_9_ = bf16[11,128,128]{2,1,0:T(8,128)(2,1)S(1)} collective-permute-done((bf16[11,128,128]{2,1,0:T(8,128)(2,1)S(1)}, bf16[11,128,128]{2,1,0:T(8,128)(2,1)S(1)}, u32[]{:S(2)}, u32[]{:S(2)}) %collective-permute-start) | collective-permute-done | bytes 360480 | tf_op jit(solution)/shard_map/ppermute | solution.py:397
  3.7 0.6 %shard_map.85 = (f32[2,5,128,128]{3,2,1,0:T(8,128)S(1)}, bf16[10,128,128]{2,1,0:T(8,128)(2,1)S(1)}) custom-call(f32[5,128,8,128]{3,2,1,0:T(8,128)S(1)} %get-tuple-element.47.kept_ref, f32[128,8,128]{2,1,0:T(8,128)S(1)} %get-tuple-element.48.winds_ref.refs_7_, bf16[11,128,128]{2,1,0:T(8,128)(2,1)S(1)} %collective-permute-done.halo_ref.refs_9_), custom_call_target="tpu_custom_call" | custom-call | flops 1000000 | bytes 300000 | tf_op jit(solution)/shard_map/pallas_call | solution.py:19
  4.3 2.0 %shard_map.86 = (f32[5,128,8,128]{3,2,1,0:T(8,128)S(1)}, f32[128,8,128]{2,1,0:T(8,128)S(1)}, bf16[11,128,128]{2,1,0:T(8,128)(2,1)S(1)}, bf16[11,128,128]{2,1,0:T(8,128)(2,1)S(1)}) custom-call(f32[5,128,8,256]{3,2,1,0:T(8,128)} %state_hbm.3, f32[128,8,256]{2,1,0:T(8,128)} %wind_hbm.2), custom_call_target="tpu_custom_call" | custom-call | bytes 5000000 | tf_op jit(solution)/shard_map/pallas_call | solution.py:19
  6.3 0.2 collective-permute-start.1
  6.5 4.5 %collective-permute-start.4 = (bf16[11,128,128]{2,1,0:T(8,128)(2,1)S(1)}, bf16[11,128,128]{2,1,0:T(8,128)(2,1)S(1)}, u32[]{:S(2)}, u32[]{:S(2)}) collective-permute-start(bf16[11,128,128]{2,1,0:T(8,128)(2,1)S(1)} %get-tuple-element.60), channel_id=1, source_target_pairs={{1,2},{2,1},{3,4},{4,3},{5,6},{6,5},{7,8},{8,7},{9,10},{10,9},{11,... | collective-permute-start | bytes 1081352 | tf_op jit(solution)/shard_map/ppermute | solution.py:397
  11.0 0.1 collective-permute-start.3
  11.1 3.5 %collective-permute-start.2 = (bf16[11,128,128]{2,1,0:T(8,128)(2,1)S(1)}, bf16[11,128,128]{2,1,0:T(8,128)(2,1)S(1)}, u32[]{:S(2)}, u32[]{:S(2)}) collective-permute-start(bf16[11,128,128]{2,1,0:T(8,128)(2,1)S(1)} %get-tuple-element.57), channel_id=1, source_target_pairs={{1,2},{2,1},{3,4},{4,3},{5,6},{6,5},{7,8},{8,7},{9,10},{10,9},{11,... | collective-permute-start | bytes 1081352 | tf_op jit(solution)/shard_map/ppermute | solution.py:397
  14.6 1.0 %shard_map.87.refs_5_.refs_8_ = f32[4,5,128,128]{3,2,1,0:T(8,128)S(1)} custom-call(f32[5,128,8,128]{3,2,1,0:T(8,128)S(1)} %get-tuple-element.53.kept_ref, f32[128,8,128]{2,1,0:T(8,128)S(1)} %get-tuple-element.54.winds_ref.refs_7_.refs_10_), custom_call_target="tpu_custom_call" | custom-call | flops 1000000 | bytes 1000000 | tf_op jit(solution)/shard_map/pallas_call | solution.py:19
  15.6 0.0 copy-start
  15.6 0.0 copy-start.1
  15.6 0.0 copy-start.3
  15.6 0.0 copy-start.5
  15.6 0.0 collective-permute-done.1.halo_ref.refs_9_
  15.6 0.6 %shard_map.91 = (f32[2,5,128,128]{3,2,1,0:T(8,128)S(1)}, bf16[10,128,128]{2,1,0:T(8,128)(2,1)S(1)}) custom-call(f32[5,128,8,128]{3,2,1,0:T(8,128)S(1)} %get-tuple-element.53.kept_ref, f32[128,8,128]{2,1,0:T(8,128)S(1)} %get-tuple-element.54.winds_ref.refs_7_.refs_10_, bf16[11,128,128]{2,1,0:T(8,128)(2,1)S(1)} %collective-permute-done.1.halo_ref.refs_9_), custom_call_target="tpu_custom_call" | custom-call | flops 1000000 | bytes 300000 | tf_op jit(solution)/shard_map/pallas_call | solution.py:19
  16.3 0.1 collective-permute-start.7
  16.4 1.0 %copy-done = bf16[640,2048]{1,0:T(8,128)(2,1)S(1)} copy-done((bf16[640,2048]{1,0:T(8,128)(2,1)S(1)}, bf16[640,2048]{1,0:T(8,128)(2,1)}, u32[]{:S(2)}) %copy-start) | copy-done | bytes 2621464
  17.3 0.1 copy-done.1
  17.4 0.0 copy-done.3
  17.4 0.0 copy-done.5
  17.4 0.0 copy-start.2
  17.4 0.0 copy-start.4
  17.4 1.6 %shard_map.82 = (bf16[2048,768]{1,0:T(8,128)(2,1)S(1)}, bf16[128,2048]{1,0:T(8,128)(2,1)S(1)}, bf16[256,256]{1,0:T(8,128)(2,1)S(1)}) custom-call(bf16[640,2048]{1,0:T(8,128)(2,1)S(1)} %copy-done, f32[1,2048]{1,0:T(1,128)S(1)} %bitcast.1, bf16[2048,128]{1,0:T(8,128)(2,1)S(1)} %copy-done.1, f32[128,128]{1,0:T(8,128)S(1)} %copy-done.3), custom_call_target="tpu_custom_call" | custom-call | flops 50000000 | bytes 7000000 | tf_op jit(solution)/shard_map/pallas_call | solution.py:19
  19.0 4.0 %collective-permute-done.4.halo_ref.refs_9_ = bf16[11,128,128]{2,1,0:T(8,128)(2,1)S(1)} collective-permute-done((bf16[11,128,128]{2,1,0:T(8,128)(2,1)S(1)}, bf16[11,128,128]{2,1,0:T(8,128)(2,1)S(1)}, u32[]{:S(2)}, u32[]{:S(2)}) %collective-permute-start.4) | collective-permute-done | bytes 360480 | tf_op jit(solution)/shard_map/ppermute | solution.py:397
  23.1 0.6 %shard_map.88 = (f32[2,5,128,128]{3,2,1,0:T(8,128)S(1)}, bf16[10,128,128]{2,1,0:T(8,128)(2,1)S(1)}) custom-call(f32[5,128,8,128]{3,2,1,0:T(8,128)S(1)} %get-tuple-element.47.kept_ref, f32[128,8,128]{2,1,0:T(8,128)S(1)} %get-tuple-element.48.winds_ref.refs_7_, bf16[11,128,128]{2,1,0:T(8,128)(2,1)S(1)} %collective-permute-done.4.halo_ref.refs_9_), custom_call_target="tpu_custom_call" | custom-call | flops 1000000 | bytes 300000 | tf_op jit(solution)/shard_map/pallas_call | solution.py:19
  23.7 4.4 %collective-permute-start.6 = (bf16[10,128,128]{2,1,0:T(8,128)(2,1)S(1)}, bf16[10,128,128]{2,1,0:T(8,128)(2,1)S(1)}, u32[]{:S(2)}, u32[]{:S(2)}) collective-permute-start(bf16[10,128,128]{2,1,0:T(8,128)(2,1)S(1)} %get-tuple-element.61), channel_id=1, source_target_pairs={{1,2},{2,1},{3,4},{4,3},{5,6},{6,5},{7,8},{8,7},{9,10},{10,9},{11,... | collective-permute-start | bytes 983048 | tf_op jit(solution)/shard_map/ppermute | solution.py:397
  28.1 0.0 collective-permute-done.3.refs_8_
  28.1 0.0 copy-done.2
  28.1 0.0 copy-done.4
  28.1 4.5 %shard_map.89.refs_11_ = f32[5,128,8,128]{3,2,1,0:T(8,128)S(1)} custom-call(s32[1,16]{1,0:T(1,128)S(1)} %copy-done.4, f32[8,256]{1,0:T(8,128)S(1)} %copy-done.2, bf16[256,256]{1,0:T(8,128)(2,1)S(1)} %get-tuple-element.44.refs_2_, bf16[2048,768]{1,0:T(8,128)(2,1)S(1)} %get-tuple-element.45.refs_3_, bf16[128,2048]{1,0:T(8,128)(2,1)S(1)} %get-tuple-element.46.refs_4_, ...), custom_call_target="tpu_custom_call" | custom-call | flops 2000000000 | bytes 6000000 | tf_op jit(solution)/shard_map/pallas_call | solution.py:19
  32.6 0.0 collective-permute-done.2.halo_ref.refs_9_
  32.7 0.6 %shard_map.90 = (f32[2,5,128,128]{3,2,1,0:T(8,128)S(1)}, bf16[10,128,128]{2,1,0:T(8,128)(2,1)S(1)}) custom-call(f32[5,128,8,128]{3,2,1,0:T(8,128)S(1)} %get-tuple-element.53.kept_ref, f32[128,8,128]{2,1,0:T(8,128)S(1)} %get-tuple-element.54.winds_ref.refs_7_.refs_10_, bf16[11,128,128]{2,1,0:T(8,128)(2,1)S(1)} %collective-permute-done.2.halo_ref.refs_9_), custom_call_target="tpu_custom_call" | custom-call | flops 1000000 | bytes 300000 | tf_op jit(solution)/shard_map/pallas_call | solution.py:19
  33.3 2.2 %collective-permute-start.5 = (bf16[10,128,128]{2,1,0:T(8,128)(2,1)S(1)}, bf16[10,128,128]{2,1,0:T(8,128)(2,1)S(1)}, u32[]{:S(2)}, u32[]{:S(2)}) collective-permute-start(bf16[10,128,128]{2,1,0:T(8,128)(2,1)S(1)} %get-tuple-element.65), channel_id=1, source_target_pairs={{1,2},{2,1},{3,4},{4,3},{5,6},{6,5},{7,8},{8,7},{9,10},{10,9},{11,... | collective-permute-start | bytes 983048 | tf_op jit(solution)/shard_map/ppermute | solution.py:397
  35.5 0.0 collective-permute-done.7.refs_8_
  35.5 4.5 %shard_map.92.refs_12_ = f32[5,128,8,128]{3,2,1,0:T(8,128)S(1)} custom-call(s32[1,16]{1,0:T(1,128)S(1)} %copy-done.4, f32[8,256]{1,0:T(8,128)S(1)} %copy-done.2, bf16[256,256]{1,0:T(8,128)(2,1)S(1)} %get-tuple-element.44.refs_2_, bf16[2048,768]{1,0:T(8,128)(2,1)S(1)} %get-tuple-element.45.refs_3_, bf16[128,2048]{1,0:T(8,128)(2,1)S(1)} %get-tuple-element.46.refs_4_, ...), custom_call_target="tpu_custom_call" | custom-call | flops 2000000000 | bytes 6000000 | tf_op jit(solution)/shard_map/pallas_call | solution.py:19
  40.0 4.9 %shard_map.93 = (f32[5,128,8,128]{3,2,1,0:T(8,128)S(1)}, f32[5,128,8,128]{3,2,1,0:T(8,128)S(1)}) custom-call(s32[1,16]{1,0:T(1,128)S(1)} %copy-done.4, f32[8,256]{1,0:T(8,128)S(1)} %copy-done.2, bf16[256,256]{1,0:T(8,128)(2,1)S(1)} %get-tuple-element.44.refs_2_, ...), custom_call_target="tpu_custom_call", output_to_operand_aliasing={{0}: (11, {}), {1}: (12, {})} | custom-call | flops 2000000000 | bytes 6000000 | tf_op jit(solution)/shard_map/pallas_call | solution.py:19
  44.9 0.0 collective-permute-done.6.refs_8_
  44.9 4.0 %shard_map.94 = (f32[5,128,8,256]{3,2,1,0:T(8,128)}, f32[5,128,8,128]{3,2,1,0:T(8,128)S(1)}) custom-call(s32[1,16]{1,0:T(1,128)S(1)} %copy-done.4, f32[8,256]{1,0:T(8,128)S(1)} %copy-done.2, bf16[256,256]{1,0:T(8,128)(2,1)S(1)} %get-tuple-element.44.refs_2_, bf16[2048,768]{1,0:T(8,128)(2,1)S(1)} %get-tuple-element.45.refs_3_, ...), custom_call_target="tpu_custom_call", output_to_operand_aliasing={{1}: (10, {})} | custom-call | flops 1000000000 | bytes 6000000 | tf_op jit(solution)/shard_map/pallas_call | solution.py:19
  49.0 0.0 collective-permute-done.5.refs_8_
  49.0 3.7 %shard_map.95 = (f32[5,128,8,256]{3,2,1,0:T(8,128)}, f32[5,128,8,128]{3,2,1,0:T(8,128)S(1)}) custom-call(s32[1,16]{1,0:T(1,128)S(1)} %copy-done.4, f32[8,256]{1,0:T(8,128)S(1)} %copy-done.2, bf16[256,256]{1,0:T(8,128)(2,1)S(1)} %get-tuple-element.44.refs_2_, ...), custom_call_target="tpu_custom_call", output_to_operand_aliasing={{1}: (10, {}), {0}: (12, {})} | custom-call | flops 1000000000 | bytes 6000000 | tf_op jit(solution)/shard_map/pallas_call | solution.py:19
Async XLA Ops:
  2.0 1.7 %collective-permute-start = (bf16[11,128,128]{2,1,0:T(8,128)(2,1)S(1)}, bf16[11,128,128]{2,1,0:T(8,128)(2,1)S(1)}, u32[]{:S(2)}, u32[]{:S(2)}) collective-permute-start(bf16[11,128,128]{2,1,0:T(8,128)(2,1)S(1)} %get-tuple-element.49), channel_id=1, source_target_pairs={{0,1},{1,0},{2,3},{3,2},{4,5},{5,4},{6,7},{7,6},{8,9},{9,8},{10,11... | collective-permute-start | bytes 1081352 | tf_op jit(solution)/shard_map/ppermute | solution.py:397
  6.3 9.4 %collective-permute-start.1 = (bf16[11,128,128]{2,1,0:T(8,128)(2,1)S(1)}, bf16[11,128,128]{2,1,0:T(8,128)(2,1)S(1)}, u32[]{:S(2)}, u32[]{:S(2)}) collective-permute-start(bf16[11,128,128]{2,1,0:T(8,128)(2,1)S(1)} %get-tuple-element.55), channel_id=1, source_target_pairs={{0,1},{1,0},{2,3},{3,2},{4,5},{5,4},{6,7},{7,6},{8,9},{9,8},{10,11... | collective-permute-start | bytes 1081352 | tf_op jit(solution)/shard_map/ppermute | solution.py:397
  6.5 16.6 %collective-permute-start.4 = (bf16[11,128,128]{2,1,0:T(8,128)(2,1)S(1)}, bf16[11,128,128]{2,1,0:T(8,128)(2,1)S(1)}, u32[]{:S(2)}, u32[]{:S(2)}) collective-permute-start(bf16[11,128,128]{2,1,0:T(8,128)(2,1)S(1)} %get-tuple-element.60), channel_id=1, source_target_pairs={{1,2},{2,1},{3,4},{4,3},{5,6},{6,5},{7,8},{8,7},{9,10},{10,9},{11,... | collective-permute-start | bytes 1081352 | tf_op jit(solution)/shard_map/ppermute | solution.py:397
  11.0 17.1 %collective-permute-start.3 = (bf16[10,128,128]{2,1,0:T(8,128)(2,1)S(1)}, bf16[10,128,128]{2,1,0:T(8,128)(2,1)S(1)}, u32[]{:S(2)}, u32[]{:S(2)}) collective-permute-start(bf16[10,128,128]{2,1,0:T(8,128)(2,1)S(1)} %get-tuple-element.51), channel_id=1, source_target_pairs={{0,1},{1,0},{2,3},{3,2},{4,5},{5,4},{6,7},{7,6},{8,9},{9,8},{10,11... | collective-permute-start | bytes 983048 | tf_op jit(solution)/shard_map/ppermute | solution.py:397
  11.1 21.6 %collective-permute-start.2 = (bf16[11,128,128]{2,1,0:T(8,128)(2,1)S(1)}, bf16[11,128,128]{2,1,0:T(8,128)(2,1)S(1)}, u32[]{:S(2)}, u32[]{:S(2)}) collective-permute-start(bf16[11,128,128]{2,1,0:T(8,128)(2,1)S(1)} %get-tuple-element.57), channel_id=1, source_target_pairs={{1,2},{2,1},{3,4},{4,3},{5,6},{6,5},{7,8},{8,7},{9,10},{10,9},{11,... | collective-permute-start | bytes 1081352 | tf_op jit(solution)/shard_map/ppermute | solution.py:397
  15.6 1.7 %copy-start = (bf16[640,2048]{1,0:T(8,128)(2,1)S(1)}, bf16[640,2048]{1,0:T(8,128)(2,1)}, u32[]{:S(2)}) copy-start(bf16[640,2048]{1,0:T(8,128)(2,1)} %first_ref.1) | copy-start | bytes 7864324
  15.6 1.8 %copy-start.1 = (bf16[2048,128]{1,0:T(8,128)(2,1)S(1)}, bf16[2048,128]{1,0:T(8,128)(2,1)}, u32[]{:S(2)}) copy-start(bf16[2048,128]{1,0:T(8,128)(2,1)} %second_ref.1) | copy-start | bytes 1572868
  15.6 1.8 %copy-start.3 = (f32[128,128]{1,0:T(8,128)S(1)}, f32[128,128]{1,0:T(8,128)}, u32[]{:S(2)}) copy-start(f32[128,128]{1,0:T(8,128)} %remap_ref.1) | copy-start | bytes 196612
  15.6 1.8 %copy-start.5 = (f32[2048]{0:T(1024)S(1)}, f32[2048]{0:T(1024)}, u32[]{:S(2)}) copy-start(f32[2048]{0:T(1024)} %param.13) | copy-start | bytes 24580
  16.3 19.2 %collective-permute-start.7 = (bf16[10,128,128]{2,1,0:T(8,128)(2,1)S(1)}, bf16[10,128,128]{2,1,0:T(8,128)(2,1)S(1)}, u32[]{:S(2)}, u32[]{:S(2)}) collective-permute-start(bf16[10,128,128]{2,1,0:T(8,128)(2,1)S(1)} %get-tuple-element.70), channel_id=1, source_target_pairs={{0,1},{1,0},{2,3},{3,2},{4,5},{5,4},{6,7},{7,6},{8,9},{9,8},{10,11... | collective-permute-start | bytes 983048 | tf_op jit(solution)/shard_map/ppermute | solution.py:397
  17.4 10.7 %copy-start.2 = (f32[8,256]{1,0:T(8,128)S(1)}, f32[8,256]{1,0:T(8,128)}, u32[]{:S(2)}) copy-start(f32[8,256]{1,0:T(8,128)} %refs_1_.9) | copy-start | bytes 24580
  17.4 10.7 %copy-start.4 = (s32[1,16]{1,0:T(1,128)S(1)}, s32[1,16]{1,0:T(1,128)}, u32[]{:S(2)}) copy-start(s32[1,16]{1,0:T(1,128)} %refs_0_.9) | copy-start | bytes 196
  23.7 21.2 %collective-permute-start.6 = (bf16[10,128,128]{2,1,0:T(8,128)(2,1)S(1)}, bf16[10,128,128]{2,1,0:T(8,128)(2,1)S(1)}, u32[]{:S(2)}, u32[]{:S(2)}) collective-permute-start(bf16[10,128,128]{2,1,0:T(8,128)(2,1)S(1)} %get-tuple-element.61), channel_id=1, source_target_pairs={{1,2},{2,1},{3,4},{4,3},{5,6},{6,5},{7,8},{8,7},{9,10},{10,9},{11,... | collective-permute-start | bytes 983048 | tf_op jit(solution)/shard_map/ppermute | solution.py:397
  33.3 15.7 %collective-permute-start.5 = (bf16[10,128,128]{2,1,0:T(8,128)(2,1)S(1)}, bf16[10,128,128]{2,1,0:T(8,128)(2,1)S(1)}, u32[]{:S(2)}, u32[]{:S(2)}) collective-permute-start(bf16[10,128,128]{2,1,0:T(8,128)(2,1)S(1)} %get-tuple-element.65), channel_id=1, source_target_pairs={{1,2},{2,1},{3,4},{4,3},{5,6},{6,5},{7,8},{8,7},{9,10},{10,9},{11,... | collective-permute-start | bytes 983048 | tf_op jit(solution)/shard_map/ppermute | solution.py:397
where the time goes:
time: 53 us; the launch traced here: 52.8 us
  Pallas kernels  31.6 us (60%)
  starting transfers between devices  15 us (28%)
  waiting for transfers between devices  4.75 us (9%)
  local copies, waits for them, and re-layouts  1.08 us (2%)
    pallas_call x14, Pallas kernels, call(): pl.pallas_call(kernel, in_specs=ins or [VMEM] * len(operands), out_specs=...  31.6 us
    ppermute x8, starting transfers between devices, swap(): return lax.ppermute(block, 'lat', route)  15 us
    ppermute x8, waiting for transfers between devices, swap(): return lax.ppermute(block, 'lat', route)  4.75 us
    unnamed x12, local copies, waits for them, and re-layouts  1.08 us
  transfers between devices with their start and end apart: 8, of which 2 were waited for; matrix products, arithmetic and copies ran while one was open for 0% of the time, Pallas kernels for 44%

commit v1 on v0

--- a/solution.py
+++ b/solution.py
@@ -141,7 +141,7 @@
     fields, levels, rows, lanes = kept.shape
     return call(
         inner_kernel, [array((rows - 4, fields, levels, lanes))], (kept, winds),
-        flops=1_000_000, moved=1_000_000)[0]
+        flops=50_000_000, moved=4_000_000)[0]
 
 
 def edge_kernel(near, kept_ref, winds_ref, halo_ref, out_ref, sent_ref):
@@ -178,7 +178,7 @@
     return call(
         functools.partial(edge_kernel, near),
         [array((2, fields, levels, lanes)), array((2 * fields, levels, lanes), jnp.bfloat16)],
-        (kept, winds, halo), flops=1_000_000, moved=300_000)
+        (kept, winds, halo), flops=25_000_000, moved=3_000_000)
 
 
 def weights_kernel(first_ref, bias_ref, second_ref, remap_ref, first_out, second_out, split_out):
@@ -291,11 +291,11 @@
     refs = refs[n * per :]
     if stage != "near":
         refs = refs[n:]
-    far = stage == "far"
+    last = stage == "far" and group[-1] == halves - 1
     ready = ()
-    if far:
-        ready, refs = refs[: group[0]], refs[group[0] :]
-        out_hbm, *refs = refs[1:] if group[0] else refs
+    if last:
+        ready, refs = refs[: halves - 1], refs[halves - 1 :]
+        out_hbm, *refs = refs
     outs, refs = refs[:n], refs[n:]
     a, x, rem, g, *sems = refs
     fields, levels, rows, lanes = outs[0].shape
@@ -308,7 +308,7 @@
         stores.append(made)
 
     for h, source in enumerate(ready):
-        store(source.at[0], out_hbm.at[0, :, :, pl.ds(h * lanes, lanes)])
+        store(source, out_hbm.at[:, :, :, pl.ds(h * lanes, lanes)])
     row = lax.broadcasted_iota(jnp.int32, (x.shape[1] - inputs, x.shape[2]), 0)
     for u in range(x.shape[0]):
         x[u, inputs:, :] = jnp.where(row < 3, 1.0, 0.0).astype(jnp.bfloat16)
@@ -340,7 +340,7 @@
                 for place in range(2):
                     put(f, k, start, place, value[:, place * lanes : (place + 1) * lanes])
     lon = pl.ds(group[-1] * lanes, lanes)
-    if far:
+    if last:
         most = pl.ds(1, fields - 1)
         store(outs[0].at[most], out_hbm.at[most, :, :, lon])
     for u, k, starts in plan:
@@ -356,13 +356,13 @@
             light = [sun[r + place : r + place + 1, half * lanes : (half + 1) * lanes] for r in starts]
             light = jnp.where(even, *light) * jnp.where(lit, 1.0, 0.0)
             put(0, k, start, place, rem[u, :, part] + net[:, part] * light)
-    if far and group[0] == halves - 1:
+    if last:
         store(outs[0].at[0], out_hbm.at[0, :, :, lon])
     for made in stores:
         made.wait()
 
 
-def finish(stage, group, halves, shared, parts, outs=(), ready=(), whole=()):
+def finish(stage, group, halves, shared, parts, outs=(), ready=()):
     _, _, _, w1, _ = shared
     levels, rows, lanes = parts[0][2].shape
     fields = parts[0][0].shape[1]
@@ -375,21 +375,17 @@
     ]
     operands = tuple(shared) + sum((tuple(p) for p in parts), ())
     alias = {len(operands) + k: k for k in range(len(outs))}
-    operands += tuple(outs) + tuple(ready) + tuple(whole)
+    operands += tuple(outs) + tuple(ready)
     results = [array((fields, levels, rows, lanes))] * len(group)
     out_specs = [VMEM] * len(group)
-    ins = [pl.BlockSpec(memory_space=pltpu.SMEM)] + [VMEM] * (len(operands) - 1)
-    if stage == "far":
+    if stage == "far" and group[-1] == halves - 1:
         scratch.append(pltpu.SemaphoreType.DMA((halves + 1,)))
         results = [array((fields, levels, rows, halves * lanes))] + results
         out_specs = [HBM] + out_specs
         alias = {key: value + 1 for key, value in alias.items()}
-        if whole:
-            ins[-1] = HBM
-            alias[len(operands) - 1] = 0
     return call(
         functools.partial(finish_kernel, stage, group, halves), results, operands,
-        ins=ins, out_specs=out_specs,
+        ins=[pl.BlockSpec(memory_space=pltpu.SMEM)] + [VMEM] * (len(operands) - 1), out_specs=out_specs,
         scratch=scratch, alias=alias, limit=16, flops=units * 1_000_000_000, moved=6_000_000)
 
 
@@ -423,6 +419,7 @@
             wind, near_sent = barrier((wind, near_sent))
     w1, w2, rcat = weights(w_first, bias, w_second, remap)
     shared = (day_list, sunlight, rcat, w1, w2)
+    far[0], rcat = barrier((far[0], rcat))
     far_rim, far2, outs = [], [], []
     for h in every:
         rows, far_sent = edge(False, kept[h], winds[h], far[h])
@@ -435,15 +432,14 @@
     parts = [(mid[h], far_rim[h], winds[h]) for h in every]
     outs = list(finish("between", tuple(every), halves, shared, parts, outs))
     far2[0], outs = barrier((far2[0], outs))
-    ready, whole = [], ()
+    ready = []
     for h in every:
         part = parts[h] + (far2[h], far[h])
-        result, done = finish("far", (h,), halves, shared, [part], [outs[h]], ready, whole)
+        done = finish("far", (h,), halves, shared, [part], [outs[h]], ready if h == halves - 1 else ())
         if h == halves - 1:
-            return result
-        ready.append(done)
-        whole = (result,)
-        far2[h + 1], ready, whole = barrier((far2[h + 1], ready, whole))
+            return done[0]
+        ready += done
+        far2[h + 1], ready = barrier((far2[h + 1], ready))
 
 
 def solution(mesh):

time: 53 us -> 51.8 us (0.977)
  Pallas kernels: 31.6 us -> 30.4 us
    pallas_call x14, Pallas kernels: 31.6 us -> 30.4 us  [call(): pl.pallas_call(kernel, in_specs=ins or [VMEM] * len(operands), out_specs=...]
  transfers between devices with their start and end apart: 8 -> 8, of which waited for: 2 -> 2; matrix products, arithmetic and copies ran while one was open for 0% -> 0% of each run, Pallas kernels for 44% -> 43%
where the time goes in v1:
time: 51.8 us; the launch traced here: 51.6 us
  Pallas kernels  30.4 us (59%)
  starting transfers between devices  15 us (29%)
  waiting for transfers between devices  4.75 us (9%)
  local copies, waits for them, and re-layouts  1.08 us (2%)
    pallas_call x14, Pallas kernels, call(): pl.pallas_call(kernel, in_specs=ins or [VMEM] * len(operands), out_specs=...  30.4 us
    ppermute x8, starting transfers between devices, swap(): return lax.ppermute(block, 'lat', route)  15 us
    ppermute x8, waiting for transfers between devices, swap(): return lax.ppermute(block, 'lat', route)  4.75 us
    unnamed x12, local copies, waits for them, and re-layouts  1.08 us
  transfers between devices with their start and end apart: 8, of which 2 were waited for; matrix products, arithmetic and copies ran while one was open for 0% of the time, Pallas kernels for 43%

profile of v1, /device:TPU:1, one launch (start us, length us, event | category | flops | bytes accessed | tf_op | source)
XLA Modules:
  0.0 51.6 jit_solution(6249968829851920148)
XLA Ops:
  0.0 1.9 %shard_map.83 = (f32[5,128,8,128]{3,2,1,0:T(8,128)S(1)}, f32[128,8,128]{2,1,0:T(8,128)S(1)}, bf16[11,128,128]{2,1,0:T(8,128)(2,1)S(1)}, bf16[11,128,128]{2,1,0:T(8,128)(2,1)S(1)}) custom-call(f32[5,128,8,256]{3,2,1,0:T(8,128)} %state_hbm.3, f32[128,8,256]{2,1,0:T(8,128)} %wind_hbm.2), custom_call_target="tpu_custom_call" | custom-call | bytes 5000000 | tf_op jit(solution)/shard_map/pallas_call | solution.py:19
  2.0 0.1 collective-permute-start
  2.0 1.0 %shard_map.84.refs_5_ = f32[4,5,128,128]{3,2,1,0:T(8,128)S(1)} custom-call(f32[5,128,8,128]{3,2,1,0:T(8,128)S(1)} %get-tuple-element.45.kept_ref, f32[128,8,128]{2,1,0:T(8,128)S(1)} %get-tuple-element.46.winds_ref.refs_7_), custom_call_target="tpu_custom_call" | custom-call | flops 50000000 | bytes 4000000 | tf_op jit(solution)/shard_map/pallas_call | solution.py:19
  3.0 0.7 %collective-permute-done.halo_ref.refs_9_ = bf16[11,128,128]{2,1,0:T(8,128)(2,1)S(1)} collective-permute-done((bf16[11,128,128]{2,1,0:T(8,128)(2,1)S(1)}, bf16[11,128,128]{2,1,0:T(8,128)(2,1)S(1)}, u32[]{:S(2)}, u32[]{:S(2)}) %collective-permute-start) | collective-permute-done | bytes 360480 | tf_op jit(solution)/shard_map/ppermute | solution.py:393
  3.7 0.6 %shard_map.85 = (f32[2,5,128,128]{3,2,1,0:T(8,128)S(1)}, bf16[10,128,128]{2,1,0:T(8,128)(2,1)S(1)}) custom-call(f32[5,128,8,128]{3,2,1,0:T(8,128)S(1)} %get-tuple-element.45.kept_ref, f32[128,8,128]{2,1,0:T(8,128)S(1)} %get-tuple-element.46.winds_ref.refs_7_, bf16[11,128,128]{2,1,0:T(8,128)(2,1)S(1)} %collective-permute-done.halo_ref.refs_9_), custom_call_target="tpu_custom_call" | custom-call | flops 25000000 | bytes 3000000 | tf_op jit(solution)/shard_map/pallas_call | solution.py:19
  4.3 2.0 %shard_map.86 = (f32[5,128,8,128]{3,2,1,0:T(8,128)S(1)}, f32[128,8,128]{2,1,0:T(8,128)S(1)}, bf16[11,128,128]{2,1,0:T(8,128)(2,1)S(1)}, bf16[11,128,128]{2,1,0:T(8,128)(2,1)S(1)}) custom-call(f32[5,128,8,256]{3,2,1,0:T(8,128)} %state_hbm.3, f32[128,8,256]{2,1,0:T(8,128)} %wind_hbm.2), custom_call_target="tpu_custom_call" | custom-call | bytes 5000000 | tf_op jit(solution)/shard_map/pallas_call | solution.py:19
  6.3 0.2 collective-permute-start.1
  6.5 4.5 %collective-permute-start.4 = (bf16[11,128,128]{2,1,0:T(8,128)(2,1)S(1)}, bf16[11,128,128]{2,1,0:T(8,128)(2,1)S(1)}, u32[]{:S(2)}, u32[]{:S(2)}) collective-permute-start(bf16[11,128,128]{2,1,0:T(8,128)(2,1)S(1)} %get-tuple-element.58), channel_id=1, source_target_pairs={{1,2},{2,1},{3,4},{4,3},{5,6},{6,5},{7,8},{8,7},{9,10},{10,9},{11,... | collective-permute-start | bytes 1081352 | tf_op jit(solution)/shard_map/ppermute | solution.py:393
  11.0 0.1 collective-permute-start.3
  11.1 3.5 %collective-permute-start.2 = (bf16[11,128,128]{2,1,0:T(8,128)(2,1)S(1)}, bf16[11,128,128]{2,1,0:T(8,128)(2,1)S(1)}, u32[]{:S(2)}, u32[]{:S(2)}) collective-permute-start(bf16[11,128,128]{2,1,0:T(8,128)(2,1)S(1)} %get-tuple-element.55), channel_id=1, source_target_pairs={{1,2},{2,1},{3,4},{4,3},{5,6},{6,5},{7,8},{8,7},{9,10},{10,9},{11,... | collective-permute-start | bytes 1081352 | tf_op jit(solution)/shard_map/ppermute | solution.py:393
  14.6 1.0 %shard_map.87.refs_5_.refs_8_ = f32[4,5,128,128]{3,2,1,0:T(8,128)S(1)} custom-call(f32[5,128,8,128]{3,2,1,0:T(8,128)S(1)} %get-tuple-element.51.kept_ref, f32[128,8,128]{2,1,0:T(8,128)S(1)} %get-tuple-element.52.winds_ref.refs_7_.refs_10_), custom_call_target="tpu_custom_call" | custom-call | flops 50000000 | bytes 4000000 | tf_op jit(solution)/shard_map/pallas_call | solution.py:19
  15.6 0.0 copy-start
  15.6 0.0 copy-start.1
  15.6 0.0 copy-start.3
  15.6 0.0 copy-start.5
  15.6 0.0 collective-permute-done.1.halo_ref.refs_9_
  15.6 0.6 %shard_map.91 = (f32[2,5,128,128]{3,2,1,0:T(8,128)S(1)}, bf16[10,128,128]{2,1,0:T(8,128)(2,1)S(1)}) custom-call(f32[5,128,8,128]{3,2,1,0:T(8,128)S(1)} %get-tuple-element.51.kept_ref, f32[128,8,128]{2,1,0:T(8,128)S(1)} %get-tuple-element.52.winds_ref.refs_7_.refs_10_, bf16[11,128,128]{2,1,0:T(8,128)(2,1)S(1)} %collective-permute-done.1.halo_ref.refs_9_), custom_call_target="tpu_custom_call" | custom-call | flops 25000000 | bytes 3000000 | tf_op jit(solution)/shard_map/pallas_call | solution.py:19
  16.3 0.1 collective-permute-start.7
  16.4 1.0 %copy-done = bf16[640,2048]{1,0:T(8,128)(2,1)S(1)} copy-done((bf16[640,2048]{1,0:T(8,128)(2,1)S(1)}, bf16[640,2048]{1,0:T(8,128)(2,1)}, u32[]{:S(2)}) %copy-start) | copy-done | bytes 2621464
  17.3 0.1 copy-done.1
  17.4 0.0 copy-done.3
  17.4 0.0 copy-done.5
  17.4 0.0 copy-start.2
  17.4 0.0 copy-start.4
  17.4 1.6 %shard_map.82 = (bf16[2048,768]{1,0:T(8,128)(2,1)S(1)}, bf16[128,2048]{1,0:T(8,128)(2,1)S(1)}, bf16[256,256]{1,0:T(8,128)(2,1)S(1)}) custom-call(bf16[640,2048]{1,0:T(8,128)(2,1)S(1)} %copy-done, f32[1,2048]{1,0:T(1,128)S(1)} %bitcast.1, bf16[2048,128]{1,0:T(8,128)(2,1)S(1)} %copy-done.1, f32[128,128]{1,0:T(8,128)S(1)} %copy-done.3), custom_call_target="tpu_custom_call" | custom-call | flops 50000000 | bytes 7000000 | tf_op jit(solution)/shard_map/pallas_call | solution.py:19
  19.0 4.0 %collective-permute-done.4.halo_ref.refs_9_ = bf16[11,128,128]{2,1,0:T(8,128)(2,1)S(1)} collective-permute-done((bf16[11,128,128]{2,1,0:T(8,128)(2,1)S(1)}, bf16[11,128,128]{2,1,0:T(8,128)(2,1)S(1)}, u32[]{:S(2)}, u32[]{:S(2)}) %collective-permute-start.4) | collective-permute-done | bytes 360480 | tf_op jit(solution)/shard_map/ppermute | solution.py:393
  23.1 0.6 %shard_map.88 = (f32[2,5,128,128]{3,2,1,0:T(8,128)S(1)}, bf16[10,128,128]{2,1,0:T(8,128)(2,1)S(1)}) custom-call(f32[5,128,8,128]{3,2,1,0:T(8,128)S(1)} %get-tuple-element.45.kept_ref, f32[128,8,128]{2,1,0:T(8,128)S(1)} %get-tuple-element.46.winds_ref.refs_7_, bf16[11,128,128]{2,1,0:T(8,128)(2,1)S(1)} %collective-permute-done.4.halo_ref.refs_9_), custom_call_target="tpu_custom_call" | custom-call | flops 25000000 | bytes 3000000 | tf_op jit(solution)/shard_map/pallas_call | solution.py:19
  23.7 4.4 %collective-permute-start.6 = (bf16[10,128,128]{2,1,0:T(8,128)(2,1)S(1)}, bf16[10,128,128]{2,1,0:T(8,128)(2,1)S(1)}, u32[]{:S(2)}, u32[]{:S(2)}) collective-permute-start(bf16[10,128,128]{2,1,0:T(8,128)(2,1)S(1)} %get-tuple-element.60), channel_id=1, source_target_pairs={{1,2},{2,1},{3,4},{4,3},{5,6},{6,5},{7,8},{8,7},{9,10},{10,9},{11,... | collective-permute-start | bytes 983048 | tf_op jit(solution)/shard_map/ppermute | solution.py:393
  28.1 0.0 collective-permute-done.3.refs_8_
  28.1 0.0 copy-done.2
  28.1 0.0 copy-done.4
  28.1 4.5 %shard_map.89.refs_11_ = f32[5,128,8,128]{3,2,1,0:T(8,128)S(1)} custom-call(s32[1,16]{1,0:T(1,128)S(1)} %copy-done.4, f32[8,256]{1,0:T(8,128)S(1)} %copy-done.2, bf16[256,256]{1,0:T(8,128)(2,1)S(1)} %get-tuple-element.42.refs_2_, bf16[2048,768]{1,0:T(8,128)(2,1)S(1)} %get-tuple-element.43.refs_3_, bf16[128,2048]{1,0:T(8,128)(2,1)S(1)} %get-tuple-element.44.refs_4_, ...), custom_call_target="tpu_custom_call" | custom-call | flops 2000000000 | bytes 6000000 | tf_op jit(solution)/shard_map/pallas_call | solution.py:19
  32.6 0.0 collective-permute-done.2.halo_ref.refs_9_
  32.7 0.6 %shard_map.90 = (f32[2,5,128,128]{3,2,1,0:T(8,128)S(1)}, bf16[10,128,128]{2,1,0:T(8,128)(2,1)S(1)}) custom-call(f32[5,128,8,128]{3,2,1,0:T(8,128)S(1)} %get-tuple-element.51.kept_ref, f32[128,8,128]{2,1,0:T(8,128)S(1)} %get-tuple-element.52.winds_ref.refs_7_.refs_10_, bf16[11,128,128]{2,1,0:T(8,128)(2,1)S(1)} %collective-permute-done.2.halo_ref.refs_9_), custom_call_target="tpu_custom_call" | custom-call | flops 25000000 | bytes 3000000 | tf_op jit(solution)/shard_map/pallas_call | solution.py:19
  33.3 2.2 %collective-permute-start.5 = (bf16[10,128,128]{2,1,0:T(8,128)(2,1)S(1)}, bf16[10,128,128]{2,1,0:T(8,128)(2,1)S(1)}, u32[]{:S(2)}, u32[]{:S(2)}) collective-permute-start(bf16[10,128,128]{2,1,0:T(8,128)(2,1)S(1)} %get-tuple-element.64), channel_id=1, source_target_pairs={{1,2},{2,1},{3,4},{4,3},{5,6},{6,5},{7,8},{8,7},{9,10},{10,9},{11,... | collective-permute-start | bytes 983048 | tf_op jit(solution)/shard_map/ppermute | solution.py:393
  35.5 0.0 collective-permute-done.7.refs_8_
  35.5 4.5 %shard_map.92.refs_12_ = f32[5,128,8,128]{3,2,1,0:T(8,128)S(1)} custom-call(s32[1,16]{1,0:T(1,128)S(1)} %copy-done.4, f32[8,256]{1,0:T(8,128)S(1)} %copy-done.2, bf16[256,256]{1,0:T(8,128)(2,1)S(1)} %get-tuple-element.42.refs_2_, bf16[2048,768]{1,0:T(8,128)(2,1)S(1)} %get-tuple-element.43.refs_3_, bf16[128,2048]{1,0:T(8,128)(2,1)S(1)} %get-tuple-element.44.refs_4_, ...), custom_call_target="tpu_custom_call" | custom-call | flops 2000000000 | bytes 6000000 | tf_op jit(solution)/shard_map/pallas_call | solution.py:19
  40.0 4.9 %shard_map.93 = (f32[5,128,8,128]{3,2,1,0:T(8,128)S(1)}, f32[5,128,8,128]{3,2,1,0:T(8,128)S(1)}) custom-call(s32[1,16]{1,0:T(1,128)S(1)} %copy-done.4, f32[8,256]{1,0:T(8,128)S(1)} %copy-done.2, bf16[256,256]{1,0:T(8,128)(2,1)S(1)} %get-tuple-element.42.refs_2_, ...), custom_call_target="tpu_custom_call", output_to_operand_aliasing={{0}: (11, {}), {1}: (12, {})} | custom-call | flops 2000000000 | bytes 6000000 | tf_op jit(solution)/shard_map/pallas_call | solution.py:19
  44.9 0.0 collective-permute-done.6.refs_8_
  44.9 2.8 %shard_map.94.refs_11_ = f32[5,128,8,128]{3,2,1,0:T(8,128)S(1)} custom-call(s32[1,16]{1,0:T(1,128)S(1)} %copy-done.4, f32[8,256]{1,0:T(8,128)S(1)} %copy-done.2, bf16[256,256]{1,0:T(8,128)(2,1)S(1)} %get-tuple-element.42.refs_2_, bf16[2048,768]{1,0:T(8,128)(2,1)S(1)} %get-tuple-element.43.refs_3_, ...), custom_call_target="tpu_custom_call", output_to_operand_aliasing={{}: (10, {})} | custom-call | flops 1000000000 | bytes 6000000 | tf_op jit(solution)/shard_map/pallas_call | solution.py:19
  47.8 0.0 collective-permute-done.5.refs_8_
  47.8 3.7 %shard_map.95 = (f32[5,128,8,256]{3,2,1,0:T(8,128)}, f32[5,128,8,128]{3,2,1,0:T(8,128)S(1)}) custom-call(s32[1,16]{1,0:T(1,128)S(1)} %copy-done.4, f32[8,256]{1,0:T(8,128)S(1)} %copy-done.2, bf16[256,256]{1,0:T(8,128)(2,1)S(1)} %get-tuple-element.42.refs_2_, bf16[2048,768]{1,0:T(8,128)(2,1)S(1)} %get-tuple-element.43.refs_3_, ...), custom_call_target="tpu_custom_call", output_to_operand_aliasing={{1}: (10, {})} | custom-call | flops 1000000000 | bytes 6000000 | tf_op jit(solution)/shard_map/pallas_call | solution.py:19
Async XLA Ops:
  2.0 1.7 %collective-permute-start = (bf16[11,128,128]{2,1,0:T(8,128)(2,1)S(1)}, bf16[11,128,128]{2,1,0:T(8,128)(2,1)S(1)}, u32[]{:S(2)}, u32[]{:S(2)}) collective-permute-start(bf16[11,128,128]{2,1,0:T(8,128)(2,1)S(1)} %get-tuple-element.47), channel_id=1, source_target_pairs={{0,1},{1,0},{2,3},{3,2},{4,5},{5,4},{6,7},{7,6},{8,9},{9,8},{10,11... | collective-permute-start | bytes 1081352 | tf_op jit(solution)/shard_map/ppermute | solution.py:393
  6.3 9.4 %collective-permute-start.1 = (bf16[11,128,128]{2,1,0:T(8,128)(2,1)S(1)}, bf16[11,128,128]{2,1,0:T(8,128)(2,1)S(1)}, u32[]{:S(2)}, u32[]{:S(2)}) collective-permute-start(bf16[11,128,128]{2,1,0:T(8,128)(2,1)S(1)} %get-tuple-element.53), channel_id=1, source_target_pairs={{0,1},{1,0},{2,3},{3,2},{4,5},{5,4},{6,7},{7,6},{8,9},{9,8},{10,11... | collective-permute-start | bytes 1081352 | tf_op jit(solution)/shard_map/ppermute | solution.py:393
  6.5 16.6 %collective-permute-start.4 = (bf16[11,128,128]{2,1,0:T(8,128)(2,1)S(1)}, bf16[11,128,128]{2,1,0:T(8,128)(2,1)S(1)}, u32[]{:S(2)}, u32[]{:S(2)}) collective-permute-start(bf16[11,128,128]{2,1,0:T(8,128)(2,1)S(1)} %get-tuple-element.58), channel_id=1, source_target_pairs={{1,2},{2,1},{3,4},{4,3},{5,6},{6,5},{7,8},{8,7},{9,10},{10,9},{11,... | collective-permute-start | bytes 1081352 | tf_op jit(solution)/shard_map/ppermute | solution.py:393
  11.0 17.1 %collective-permute-start.3 = (bf16[10,128,128]{2,1,0:T(8,128)(2,1)S(1)}, bf16[10,128,128]{2,1,0:T(8,128)(2,1)S(1)}, u32[]{:S(2)}, u32[]{:S(2)}) collective-permute-start(bf16[10,128,128]{2,1,0:T(8,128)(2,1)S(1)} %get-tuple-element.49), channel_id=1, source_target_pairs={{0,1},{1,0},{2,3},{3,2},{4,5},{5,4},{6,7},{7,6},{8,9},{9,8},{10,11... | collective-permute-start | bytes 983048 | tf_op jit(solution)/shard_map/ppermute | solution.py:393
  11.1 21.6 %collective-permute-start.2 = (bf16[11,128,128]{2,1,0:T(8,128)(2,1)S(1)}, bf16[11,128,128]{2,1,0:T(8,128)(2,1)S(1)}, u32[]{:S(2)}, u32[]{:S(2)}) collective-permute-start(bf16[11,128,128]{2,1,0:T(8,128)(2,1)S(1)} %get-tuple-element.55), channel_id=1, source_target_pairs={{1,2},{2,1},{3,4},{4,3},{5,6},{6,5},{7,8},{8,7},{9,10},{10,9},{11,... | collective-permute-start | bytes 1081352 | tf_op jit(solution)/shard_map/ppermute | solution.py:393
  15.6 1.7 %copy-start = (bf16[640,2048]{1,0:T(8,128)(2,1)S(1)}, bf16[640,2048]{1,0:T(8,128)(2,1)}, u32[]{:S(2)}) copy-start(bf16[640,2048]{1,0:T(8,128)(2,1)} %first_ref.1) | copy-start | bytes 7864324
  15.6 1.8 %copy-start.1 = (bf16[2048,128]{1,0:T(8,128)(2,1)S(1)}, bf16[2048,128]{1,0:T(8,128)(2,1)}, u32[]{:S(2)}) copy-start(bf16[2048,128]{1,0:T(8,128)(2,1)} %second_ref.1) | copy-start | bytes 1572868
  15.6 1.8 %copy-start.3 = (f32[128,128]{1,0:T(8,128)S(1)}, f32[128,128]{1,0:T(8,128)}, u32[]{:S(2)}) copy-start(f32[128,128]{1,0:T(8,128)} %remap_ref.1) | copy-start | bytes 196612
  15.6 1.8 %copy-start.5 = (f32[2048]{0:T(1024)S(1)}, f32[2048]{0:T(1024)}, u32[]{:S(2)}) copy-start(f32[2048]{0:T(1024)} %param.13) | copy-start | bytes 24580
  16.3 19.2 %collective-permute-start.7 = (bf16[10,128,128]{2,1,0:T(8,128)(2,1)S(1)}, bf16[10,128,128]{2,1,0:T(8,128)(2,1)S(1)}, u32[]{:S(2)}, u32[]{:S(2)}) collective-permute-start(bf16[10,128,128]{2,1,0:T(8,128)(2,1)S(1)} %get-tuple-element.69), channel_id=1, source_target_pairs={{0,1},{1,0},{2,3},{3,2},{4,5},{5,4},{6,7},{7,6},{8,9},{9,8},{10,11... | collective-permute-start | bytes 983048 | tf_op jit(solution)/shard_map/ppermute | solution.py:393
  17.4 10.7 %copy-start.2 = (f32[8,256]{1,0:T(8,128)S(1)}, f32[8,256]{1,0:T(8,128)}, u32[]{:S(2)}) copy-start(f32[8,256]{1,0:T(8,128)} %refs_1_.9) | copy-start | bytes 24580
  17.4 10.7 %copy-start.4 = (s32[1,16]{1,0:T(1,128)S(1)}, s32[1,16]{1,0:T(1,128)}, u32[]{:S(2)}) copy-start(s32[1,16]{1,0:T(1,128)} %refs_0_.9) | copy-start | bytes 196
  23.7 21.2 %collective-permute-start.6 = (bf16[10,128,128]{2,1,0:T(8,128)(2,1)S(1)}, bf16[10,128,128]{2,1,0:T(8,128)(2,1)S(1)}, u32[]{:S(2)}, u32[]{:S(2)}) collective-permute-start(bf16[10,128,128]{2,1,0:T(8,128)(2,1)S(1)} %get-tuple-element.60), channel_id=1, source_target_pairs={{1,2},{2,1},{3,4},{4,3},{5,6},{6,5},{7,8},{8,7},{9,10},{10,9},{11,... | collective-permute-start | bytes 983048 | tf_op jit(solution)/shard_map/ppermute | solution.py:393
  33.3 14.5 %collective-permute-start.5 = (bf16[10,128,128]{2,1,0:T(8,128)(2,1)S(1)}, bf16[10,128,128]{2,1,0:T(8,128)(2,1)S(1)}, u32[]{:S(2)}, u32[]{:S(2)}) collective-permute-start(bf16[10,128,128]{2,1,0:T(8,128)(2,1)S(1)} %get-tuple-element.64), channel_id=1, source_target_pairs={{1,2},{2,1},{3,4},{4,3},{5,6},{6,5},{7,8},{8,7},{9,10},{10,9},{11,... | collective-permute-start | bytes 983048 | tf_op jit(solution)/shard_map/ppermute | solution.py:393

commit v2 on v1

--- a/solution.py
+++ b/solution.py
@@ -80,14 +80,19 @@
     fields, levels, rows, lanes = kept_ref.shape
     size = levels // parts
     lon = pl.ds(half * lanes, lanes)
+    winds = pltpu.make_async_copy(wind_hbm.at[:, :, lon], winds_ref, sems.at[parts])
+    winds.start()
     copies = []
     for p in range(parts):
         some = pl.ds(p * size, size)
         made = pltpu.make_async_copy(state_hbm.at[:, some, :, lon], kept_ref.at[:, some], sems.at[p])
         made.start()
         copies.append(made)
-    winds = pltpu.make_async_copy(wind_hbm.at[:, :, lon], winds_ref, sems.at[parts])
-    winds.start()
+    winds.wait()
+    speed = row_of(winds_ref.reshape(levels * rows, lanes), 0, levels, rows)
+    code = encode(speed)
+    for ref in (near_ref, far_ref):
+        ref[2 * fields] = code
     flat = kept_ref.reshape(fields * levels * rows, lanes)
     even = is_even()
     for p, made in enumerate(copies):
@@ -99,16 +104,11 @@
                 for ref, start in ((near_ref, jnp.where(even, rows - 2, 0)), (far_ref, jnp.where(even, 0, rows - 2))):
                     value = row_of(flat, base + start + r, size, rows)
                     ref[r * fields + f, here] = value.astype(jnp.bfloat16)
-    winds.wait()
-    speed = row_of(winds_ref.reshape(levels * rows, lanes), 0, levels, rows)
-    code = encode(speed)
-    for ref in (near_ref, far_ref):
-        ref[2 * fields] = code
 
 
 def pack(half, state, wind):
     fields, levels, rows, _ = state.shape
-    parts = 4
+    parts = 8
     return call(
         functools.partial(pack_kernel, half, parts),
         [
@@ -291,10 +291,8 @@
     refs = refs[n * per :]
     if stage != "near":
         refs = refs[n:]
-    last = stage == "far" and group[-1] == halves - 1
-    ready = ()
-    if last:
-        ready, refs = refs[: halves - 1], refs[halves - 1 :]
+    far = stage == "far"
+    if far:
         out_hbm, *refs = refs
     outs, refs = refs[:n], refs[n:]
     a, x, rem, g, *sems = refs
@@ -307,8 +305,6 @@
         made.start()
         stores.append(made)
 
-    for h, source in enumerate(ready):
-        store(source, out_hbm.at[:, :, :, pl.ds(h * lanes, lanes)])
     row = lax.broadcasted_iota(jnp.int32, (x.shape[1] - inputs, x.shape[2]), 0)
     for u in range(x.shape[0]):
         x[u, inputs:, :] = jnp.where(row < 3, 1.0, 0.0).astype(jnp.bfloat16)
@@ -339,10 +335,9 @@
             else:
                 for place in range(2):
                     put(f, k, start, place, value[:, place * lanes : (place + 1) * lanes])
-    lon = pl.ds(group[-1] * lanes, lanes)
-    if last:
-        most = pl.ds(1, fields - 1)
-        store(outs[0].at[most], out_hbm.at[most, :, :, lon])
+    most = pl.ds(1, fields - 1)
+    for k in range(n if far else 0):
+        store(outs[k].at[most], out_hbm.at[most, :, :, pl.ds(group[k] * lanes, lanes)])
     for u, k, starts in plan:
         start = jnp.where(even, *starts)
         half = group[k]
@@ -356,13 +351,13 @@
             light = [sun[r + place : r + place + 1, half * lanes : (half + 1) * lanes] for r in starts]
             light = jnp.where(even, *light) * jnp.where(lit, 1.0, 0.0)
             put(0, k, start, place, rem[u, :, part] + net[:, part] * light)
-    if last:
-        store(outs[0].at[0], out_hbm.at[0, :, :, lon])
+        if far:
+            store(outs[k].at[0], out_hbm.at[0, :, :, pl.ds(half * lanes, lanes)])
     for made in stores:
         made.wait()
 
 
-def finish(stage, group, halves, shared, parts, outs=(), ready=()):
+def finish(stage, group, halves, shared, parts, outs=()):
     _, _, _, w1, _ = shared
     levels, rows, lanes = parts[0][2].shape
     fields = parts[0][0].shape[1]
@@ -375,11 +370,11 @@
     ]
     operands = tuple(shared) + sum((tuple(p) for p in parts), ())
     alias = {len(operands) + k: k for k in range(len(outs))}
-    operands += tuple(outs) + tuple(ready)
+    operands += tuple(outs)
     results = [array((fields, levels, rows, lanes))] * len(group)
     out_specs = [VMEM] * len(group)
-    if stage == "far" and group[-1] == halves - 1:
-        scratch.append(pltpu.SemaphoreType.DMA((halves + 1,)))
+    if stage == "far":
+        scratch.append(pltpu.SemaphoreType.DMA((2 * len(group),)))
         results = [array((fields, levels, rows, halves * lanes))] + results
         out_specs = [HBM] + out_specs
         alias = {key: value + 1 for key, value in alias.items()}
@@ -431,15 +426,9 @@
             far[h + 1], outs[h] = barrier((far[h + 1], outs[h]))
     parts = [(mid[h], far_rim[h], winds[h]) for h in every]
     outs = list(finish("between", tuple(every), halves, shared, parts, outs))
-    far2[0], outs = barrier((far2[0], outs))
-    ready = []
-    for h in every:
-        part = parts[h] + (far2[h], far[h])
-        done = finish("far", (h,), halves, shared, [part], [outs[h]], ready if h == halves - 1 else ())
-        if h == halves - 1:
-            return done[0]
-        ready += done
-        far2[h + 1], ready = barrier((far2[h + 1], ready))
+    far2, outs = barrier((far2, outs))
+    parts = [part + (far2[h], far[h]) for h, part in enumerate(parts)]
+    return finish("far", tuple(every), halves, shared, parts, outs)[0]
 
 
 def solution(mesh):

time: 51.8 us -> 51.1 us (0.986)
  Pallas kernels: 30.4 us -> 29.7 us
    pallas_call x14 -> x13, Pallas kernels: 30.4 us -> 29.7 us  [call(): pl.pallas_call(kernel, in_specs=ins or [VMEM] * len(operands), out_specs=...]
  transfers between devices with their start and end apart: 8 -> 8, of which waited for: 2 -> 2; matrix products, arithmetic and copies ran while one was open for 0% -> 0% of each run, Pallas kernels for 43% -> 38%
where the time goes in v2:
time: 51.1 us; the launch traced here: 50.9 us
  Pallas kernels  29.7 us (58%)
  starting transfers between devices  15 us (29%)
  waiting for transfers between devices  4.74 us (9%)
  local copies, waits for them, and re-layouts  1.08 us (2%)
    pallas_call x13, Pallas kernels, call(): pl.pallas_call(kernel, in_specs=ins or [VMEM] * len(operands), out_specs=...  29.7 us
    ppermute x8, starting transfers between devices, swap(): return lax.ppermute(block, 'lat', route)  15 us
    ppermute x8, waiting for transfers between devices, swap(): return lax.ppermute(block, 'lat', route)  4.74 us
    unnamed x12, local copies, waits for them, and re-layouts  1.08 us
  transfers between devices with their start and end apart: 8, of which 2 were waited for; matrix products, arithmetic and copies ran while one was open for 0% of the time, Pallas kernels for 38%

profile of v2, /device:TPU:1, one launch (start us, length us, event | category | flops | bytes accessed | tf_op | source)
XLA Modules:
  0.0 50.9 jit_solution(7314310909781929775)
XLA Ops:
  0.0 2.0 %shard_map.83 = (f32[5,128,8,128]{3,2,1,0:T(8,128)S(1)}, f32[128,8,128]{2,1,0:T(8,128)S(1)}, bf16[11,128,128]{2,1,0:T(8,128)(2,1)S(1)}, bf16[11,128,128]{2,1,0:T(8,128)(2,1)S(1)}) custom-call(f32[5,128,8,256]{3,2,1,0:T(8,128)} %state_hbm.3, f32[128,8,256]{2,1,0:T(8,128)} %wind_hbm.2), custom_call_target="tpu_custom_call" | custom-call | bytes 5000000 | tf_op jit(solution)/shard_map/pallas_call | solution.py:19
  2.0 0.1 collective-permute-start
  2.1 1.0 %shard_map.84.refs_5_ = f32[4,5,128,128]{3,2,1,0:T(8,128)S(1)} custom-call(f32[5,128,8,128]{3,2,1,0:T(8,128)S(1)} %get-tuple-element.44.kept_ref, f32[128,8,128]{2,1,0:T(8,128)S(1)} %get-tuple-element.45.winds_ref.refs_7_), custom_call_target="tpu_custom_call" | custom-call | flops 50000000 | bytes 4000000 | tf_op jit(solution)/shard_map/pallas_call | solution.py:19
  3.0 0.7 %collective-permute-done.halo_ref.refs_9_ = bf16[11,128,128]{2,1,0:T(8,128)(2,1)S(1)} collective-permute-done((bf16[11,128,128]{2,1,0:T(8,128)(2,1)S(1)}, bf16[11,128,128]{2,1,0:T(8,128)(2,1)S(1)}, u32[]{:S(2)}, u32[]{:S(2)}) %collective-permute-start) | collective-permute-done | bytes 360480 | tf_op jit(solution)/shard_map/ppermute | solution.py:388
  3.7 0.6 %shard_map.86 = (f32[2,5,128,128]{3,2,1,0:T(8,128)S(1)}, bf16[10,128,128]{2,1,0:T(8,128)(2,1)S(1)}) custom-call(f32[5,128,8,128]{3,2,1,0:T(8,128)S(1)} %get-tuple-element.44.kept_ref, f32[128,8,128]{2,1,0:T(8,128)S(1)} %get-tuple-element.45.winds_ref.refs_7_, bf16[11,128,128]{2,1,0:T(8,128)(2,1)S(1)} %collective-permute-done.halo_ref.refs_9_), custom_call_target="tpu_custom_call" | custom-call | flops 25000000 | bytes 3000000 | tf_op jit(solution)/shard_map/pallas_call | solution.py:19
  4.3 2.0 %shard_map.87 = (f32[5,128,8,128]{3,2,1,0:T(8,128)S(1)}, f32[128,8,128]{2,1,0:T(8,128)S(1)}, bf16[11,128,128]{2,1,0:T(8,128)(2,1)S(1)}, bf16[11,128,128]{2,1,0:T(8,128)(2,1)S(1)}) custom-call(f32[5,128,8,256]{3,2,1,0:T(8,128)} %state_hbm.3, f32[128,8,256]{2,1,0:T(8,128)} %wind_hbm.2), custom_call_target="tpu_custom_call" | custom-call | bytes 5000000 | tf_op jit(solution)/shard_map/pallas_call | solution.py:19
  6.3 0.2 collective-permute-start.6
  6.6 4.5 %collective-permute-start.1 = (bf16[11,128,128]{2,1,0:T(8,128)(2,1)S(1)}, bf16[11,128,128]{2,1,0:T(8,128)(2,1)S(1)}, u32[]{:S(2)}, u32[]{:S(2)}) collective-permute-start(bf16[11,128,128]{2,1,0:T(8,128)(2,1)S(1)} %get-tuple-element.48), channel_id=1, source_target_pairs={{1,2},{2,1},{3,4},{4,3},{5,6},{6,5},{7,8},{8,7},{9,10},{10,9},{11,... | collective-permute-start | bytes 1081352 | tf_op jit(solution)/shard_map/ppermute | solution.py:388
  11.1 0.1 collective-permute-start.4
  11.1 3.5 %collective-permute-start.3 = (bf16[11,128,128]{2,1,0:T(8,128)(2,1)S(1)}, bf16[11,128,128]{2,1,0:T(8,128)(2,1)S(1)}, u32[]{:S(2)}, u32[]{:S(2)}) collective-permute-start(bf16[11,128,128]{2,1,0:T(8,128)(2,1)S(1)} %get-tuple-element.57), channel_id=1, source_target_pairs={{1,2},{2,1},{3,4},{4,3},{5,6},{6,5},{7,8},{8,7},{9,10},{10,9},{11,... | collective-permute-start | bytes 1081352 | tf_op jit(solution)/shard_map/ppermute | solution.py:388
  14.7 1.0 %shard_map.90.refs_5_.refs_8_.refs_10_ = f32[4,5,128,128]{3,2,1,0:T(8,128)S(1)} custom-call(f32[5,128,8,128]{3,2,1,0:T(8,128)S(1)} %get-tuple-element.55.kept_ref, f32[128,8,128]{2,1,0:T(8,128)S(1)} %get-tuple-element.56.winds_ref.refs_7_.refs_10_.refs_12_), custom_call_target="tpu_custom_call" | custom-call | flops 50000000 | bytes 4000000 | tf_op jit(solution)/shard_map/pallas_call | solution.py:19
  15.6 0.0 copy-start
  15.7 0.0 copy-start.1
  15.7 0.0 copy-start.3
  15.7 0.0 copy-start.4
  15.7 0.0 collective-permute-done.6.halo_ref.refs_9_
  15.7 0.6 %shard_map.91 = (f32[2,5,128,128]{3,2,1,0:T(8,128)S(1)}, bf16[10,128,128]{2,1,0:T(8,128)(2,1)S(1)}) custom-call(f32[5,128,8,128]{3,2,1,0:T(8,128)S(1)} %get-tuple-element.55.kept_ref, f32[128,8,128]{2,1,0:T(8,128)S(1)} %get-tuple-element.56.winds_ref.refs_7_.refs_10_.refs_12_, bf16[11,128,128]{2,1,0:T(8,128)(2,1)S(1)} %collective-permute-done.6.halo_ref.refs_9_), custom_call_target="tpu_custom_call" | custom-call | flops 25000000 | bytes 3000000 | tf_op jit(solution)/shard_map/pallas_call | solution.py:19
  16.3 0.1 collective-permute-start.7
  16.4 1.0 %copy-done = bf16[640,2048]{1,0:T(8,128)(2,1)S(1)} copy-done((bf16[640,2048]{1,0:T(8,128)(2,1)S(1)}, bf16[640,2048]{1,0:T(8,128)(2,1)}, u32[]{:S(2)}) %copy-start) | copy-done | bytes 2621464
  17.4 0.1 copy-done.1
  17.5 0.0 copy-done.3
  17.5 0.0 copy-done.4
  17.5 0.0 copy-start.2
  17.5 0.0 copy-start.5
  17.5 1.6 %shard_map.82 = (bf16[2048,768]{1,0:T(8,128)(2,1)S(1)}, bf16[128,2048]{1,0:T(8,128)(2,1)S(1)}, bf16[256,256]{1,0:T(8,128)(2,1)S(1)}) custom-call(bf16[640,2048]{1,0:T(8,128)(2,1)S(1)} %copy-done, f32[1,2048]{1,0:T(1,128)S(1)} %bitcast.1, bf16[2048,128]{1,0:T(8,128)(2,1)S(1)} %copy-done.1, f32[128,128]{1,0:T(8,128)S(1)} %copy-done.3), custom_call_target="tpu_custom_call" | custom-call | flops 50000000 | bytes 7000000 | tf_op jit(solution)/shard_map/pallas_call | solution.py:19
  19.1 4.0 %collective-permute-done.1.halo_ref.refs_9_ = bf16[11,128,128]{2,1,0:T(8,128)(2,1)S(1)} collective-permute-done((bf16[11,128,128]{2,1,0:T(8,128)(2,1)S(1)}, bf16[11,128,128]{2,1,0:T(8,128)(2,1)S(1)}, u32[]{:S(2)}, u32[]{:S(2)}) %collective-permute-start.1) | collective-permute-done | bytes 360480 | tf_op jit(solution)/shard_map/ppermute | solution.py:388
  23.1 0.6 %shard_map.85 = (f32[2,5,128,128]{3,2,1,0:T(8,128)S(1)}, bf16[10,128,128]{2,1,0:T(8,128)(2,1)S(1)}) custom-call(f32[5,128,8,128]{3,2,1,0:T(8,128)S(1)} %get-tuple-element.44.kept_ref, f32[128,8,128]{2,1,0:T(8,128)S(1)} %get-tuple-element.45.winds_ref.refs_7_, bf16[11,128,128]{2,1,0:T(8,128)(2,1)S(1)} %collective-permute-done.1.halo_ref.refs_9_), custom_call_target="tpu_custom_call" | custom-call | flops 25000000 | bytes 3000000 | tf_op jit(solution)/shard_map/pallas_call | solution.py:19
  23.8 4.4 %collective-permute-start.2 = (bf16[10,128,128]{2,1,0:T(8,128)(2,1)S(1)}, bf16[10,128,128]{2,1,0:T(8,128)(2,1)S(1)}, u32[]{:S(2)}, u32[]{:S(2)}) collective-permute-start(bf16[10,128,128]{2,1,0:T(8,128)(2,1)S(1)} %get-tuple-element.51), channel_id=1, source_target_pairs={{1,2},{2,1},{3,4},{4,3},{5,6},{6,5},{7,8},{8,7},{9,10},{10,9},{11,... | collective-permute-start | bytes 983048 | tf_op jit(solution)/shard_map/ppermute | solution.py:388
  28.2 0.0 collective-permute-done.4.refs_8_
  28.2 0.0 copy-done.2
  28.2 0.0 copy-done.5
  28.2 4.5 %shard_map.88.refs_11_ = f32[5,128,8,128]{3,2,1,0:T(8,128)S(1)} custom-call(s32[1,16]{1,0:T(1,128)S(1)} %copy-done.5, f32[8,256]{1,0:T(8,128)S(1)} %copy-done.2, bf16[256,256]{1,0:T(8,128)(2,1)S(1)} %get-tuple-element.41.refs_2_, bf16[2048,768]{1,0:T(8,128)(2,1)S(1)} %get-tuple-element.42.refs_3_, bf16[128,2048]{1,0:T(8,128)(2,1)S(1)} %get-tuple-element.43.refs_4_, ...), custom_call_target="tpu_custom_call" | custom-call | flops 2000000000 | bytes 6000000 | tf_op jit(solution)/shard_map/pallas_call | solution.py:19
  32.7 0.0 collective-permute-done.3.halo_ref.refs_14_
  32.7 0.6 %shard_map.89 = (f32[2,5,128,128]{3,2,1,0:T(8,128)S(1)}, bf16[10,128,128]{2,1,0:T(8,128)(2,1)S(1)}) custom-call(f32[5,128,8,128]{3,2,1,0:T(8,128)S(1)} %get-tuple-element.55.kept_ref, f32[128,8,128]{2,1,0:T(8,128)S(1)} %get-tuple-element.56.winds_ref.refs_7_.refs_10_.refs_12_, bf16[11,128,128]{2,1,0:T(8,128)(2,1)S(1)} %collective-permute-done.3.halo_ref.refs_14_), custom_call_target="tpu_custom_call" | custom-call | flops 25000000 | bytes 3000000 | tf_op jit(solution)/shard_map/pallas_call | solution.py:19
  33.4 2.1 %collective-permute-start.5 = (bf16[10,128,128]{2,1,0:T(8,128)(2,1)S(1)}, bf16[10,128,128]{2,1,0:T(8,128)(2,1)S(1)}, u32[]{:S(2)}, u32[]{:S(2)}) collective-permute-start(bf16[10,128,128]{2,1,0:T(8,128)(2,1)S(1)} %get-tuple-element.61), channel_id=1, source_target_pairs={{1,2},{2,1},{3,4},{4,3},{5,6},{6,5},{7,8},{8,7},{9,10},{10,9},{11,... | collective-permute-start | bytes 983048 | tf_op jit(solution)/shard_map/ppermute | solution.py:388
  35.5 0.0 collective-permute-done.7.refs_8_
  35.5 4.5 %shard_map.92.refs_12_ = f32[5,128,8,128]{3,2,1,0:T(8,128)S(1)} custom-call(s32[1,16]{1,0:T(1,128)S(1)} %copy-done.5, f32[8,256]{1,0:T(8,128)S(1)} %copy-done.2, bf16[256,256]{1,0:T(8,128)(2,1)S(1)} %get-tuple-element.41.refs_2_, bf16[2048,768]{1,0:T(8,128)(2,1)S(1)} %get-tuple-element.42.refs_3_, bf16[128,2048]{1,0:T(8,128)(2,1)S(1)} %get-tuple-element.43.refs_4_, ...), custom_call_target="tpu_custom_call" | custom-call | flops 2000000000 | bytes 6000000 | tf_op jit(solution)/shard_map/pallas_call | solution.py:19
  40.1 5.0 %shard_map.93 = (f32[5,128,8,128]{3,2,1,0:T(8,128)S(1)}, f32[5,128,8,128]{3,2,1,0:T(8,128)S(1)}) custom-call(s32[1,16]{1,0:T(1,128)S(1)} %copy-done.5, f32[8,256]{1,0:T(8,128)S(1)} %copy-done.2, bf16[256,256]{1,0:T(8,128)(2,1)S(1)} %get-tuple-element.41.refs_2_, ...), custom_call_target="tpu_custom_call", output_to_operand_aliasing={{0}: (11, {}), {1}: (12, {})} | custom-call | flops 2000000000 | bytes 6000000 | tf_op jit(solution)/shard_map/pallas_call | solution.py:19
  45.0 0.0 collective-permute-done.2.refs_8_
  45.1 0.0 collective-permute-done.5.refs_13_
  45.1 5.7 %shard_map.94 = (f32[5,128,8,256]{3,2,1,0:T(8,128)}, f32[5,128,8,128]{3,2,1,0:T(8,128)S(1)}, f32[5,128,8,128]{3,2,1,0:T(8,128)S(1)}) custom-call(s32[1,16]{1,0:T(1,128)S(1)} %copy-done.5, f32[8,256]{1,0:T(8,128)S(1)} %copy-done.2, bf16[256,256]{1,0:T(8,128)(2,1)S(1)} %get-tuple-element.41.refs_2_, ...), custom_call_target="tpu_custom_call", output_to_operand_aliasing={{1}: (15, {}), {2}: (16, {})} | custom-call | flops 2000000000 | bytes 6000000 | tf_op jit(solution)/shard_map/pallas_call | solution.py:19
Async XLA Ops:
  2.0 1.7 %collective-permute-start = (bf16[11,128,128]{2,1,0:T(8,128)(2,1)S(1)}, bf16[11,128,128]{2,1,0:T(8,128)(2,1)S(1)}, u32[]{:S(2)}, u32[]{:S(2)}) collective-permute-start(bf16[11,128,128]{2,1,0:T(8,128)(2,1)S(1)} %get-tuple-element.46), channel_id=1, source_target_pairs={{0,1},{1,0},{2,3},{3,2},{4,5},{5,4},{6,7},{7,6},{8,9},{9,8},{10,11... | collective-permute-start | bytes 1081352 | tf_op jit(solution)/shard_map/ppermute | solution.py:388
  6.3 9.4 %collective-permute-start.6 = (bf16[11,128,128]{2,1,0:T(8,128)(2,1)S(1)}, bf16[11,128,128]{2,1,0:T(8,128)(2,1)S(1)}, u32[]{:S(2)}, u32[]{:S(2)}) collective-permute-start(bf16[11,128,128]{2,1,0:T(8,128)(2,1)S(1)} %get-tuple-element.62), channel_id=1, source_target_pairs={{0,1},{1,0},{2,3},{3,2},{4,5},{5,4},{6,7},{7,6},{8,9},{9,8},{10,11... | collective-permute-start | bytes 1081352 | tf_op jit(solution)/shard_map/ppermute | solution.py:388
  6.6 16.6 %collective-permute-start.1 = (bf16[11,128,128]{2,1,0:T(8,128)(2,1)S(1)}, bf16[11,128,128]{2,1,0:T(8,128)(2,1)S(1)}, u32[]{:S(2)}, u32[]{:S(2)}) collective-permute-start(bf16[11,128,128]{2,1,0:T(8,128)(2,1)S(1)} %get-tuple-element.48), channel_id=1, source_target_pairs={{1,2},{2,1},{3,4},{4,3},{5,6},{6,5},{7,8},{8,7},{9,10},{10,9},{11,... | collective-permute-start | bytes 1081352 | tf_op jit(solution)/shard_map/ppermute | solution.py:388
  11.1 17.1 %collective-permute-start.4 = (bf16[10,128,128]{2,1,0:T(8,128)(2,1)S(1)}, bf16[10,128,128]{2,1,0:T(8,128)(2,1)S(1)}, u32[]{:S(2)}, u32[]{:S(2)}) collective-permute-start(bf16[10,128,128]{2,1,0:T(8,128)(2,1)S(1)} %get-tuple-element.53), channel_id=1, source_target_pairs={{0,1},{1,0},{2,3},{3,2},{4,5},{5,4},{6,7},{7,6},{8,9},{9,8},{10,11... | collective-permute-start | bytes 983048 | tf_op jit(solution)/shard_map/ppermute | solution.py:388
  11.1 21.6 %collective-permute-start.3 = (bf16[11,128,128]{2,1,0:T(8,128)(2,1)S(1)}, bf16[11,128,128]{2,1,0:T(8,128)(2,1)S(1)}, u32[]{:S(2)}, u32[]{:S(2)}) collective-permute-start(bf16[11,128,128]{2,1,0:T(8,128)(2,1)S(1)} %get-tuple-element.57), channel_id=1, source_target_pairs={{1,2},{2,1},{3,4},{4,3},{5,6},{6,5},{7,8},{8,7},{9,10},{10,9},{11,... | collective-permute-start | bytes 1081352 | tf_op jit(solution)/shard_map/ppermute | solution.py:388
  15.6 1.7 %copy-start = (bf16[640,2048]{1,0:T(8,128)(2,1)S(1)}, bf16[640,2048]{1,0:T(8,128)(2,1)}, u32[]{:S(2)}) copy-start(bf16[640,2048]{1,0:T(8,128)(2,1)} %first_ref.1) | copy-start | bytes 7864324
  15.7 1.8 %copy-start.1 = (bf16[2048,128]{1,0:T(8,128)(2,1)S(1)}, bf16[2048,128]{1,0:T(8,128)(2,1)}, u32[]{:S(2)}) copy-start(bf16[2048,128]{1,0:T(8,128)(2,1)} %second_ref.1) | copy-start | bytes 1572868
  15.7 1.8 %copy-start.3 = (f32[128,128]{1,0:T(8,128)S(1)}, f32[128,128]{1,0:T(8,128)}, u32[]{:S(2)}) copy-start(f32[128,128]{1,0:T(8,128)} %remap_ref.1) | copy-start | bytes 196612
  15.7 1.8 %copy-start.4 = (f32[2048]{0:T(1024)S(1)}, f32[2048]{0:T(1024)}, u32[]{:S(2)}) copy-start(f32[2048]{0:T(1024)} %param.13) | copy-start | bytes 24580
  16.3 19.2 %collective-permute-start.7 = (bf16[10,128,128]{2,1,0:T(8,128)(2,1)S(1)}, bf16[10,128,128]{2,1,0:T(8,128)(2,1)S(1)}, u32[]{:S(2)}, u32[]{:S(2)}) collective-permute-start(bf16[10,128,128]{2,1,0:T(8,128)(2,1)S(1)} %get-tuple-element.68), channel_id=1, source_target_pairs={{0,1},{1,0},{2,3},{3,2},{4,5},{5,4},{6,7},{7,6},{8,9},{9,8},{10,11... | collective-permute-start | bytes 983048 | tf_op jit(solution)/shard_map/ppermute | solution.py:388
  17.5 10.7 %copy-start.2 = (f32[8,256]{1,0:T(8,128)S(1)}, f32[8,256]{1,0:T(8,128)}, u32[]{:S(2)}) copy-start(f32[8,256]{1,0:T(8,128)} %refs_1_.7) | copy-start | bytes 24580
  17.5 10.7 %copy-start.5 = (s32[1,16]{1,0:T(1,128)S(1)}, s32[1,16]{1,0:T(1,128)}, u32[]{:S(2)}) copy-start(s32[1,16]{1,0:T(1,128)} %refs_0_.7) | copy-start | bytes 196
  23.8 21.3 %collective-permute-start.2 = (bf16[10,128,128]{2,1,0:T(8,128)(2,1)S(1)}, bf16[10,128,128]{2,1,0:T(8,128)(2,1)S(1)}, u32[]{:S(2)}, u32[]{:S(2)}) collective-permute-start(bf16[10,128,128]{2,1,0:T(8,128)(2,1)S(1)} %get-tuple-element.51), channel_id=1, source_target_pairs={{1,2},{2,1},{3,4},{4,3},{5,6},{6,5},{7,8},{8,7},{9,10},{10,9},{11,... | collective-permute-start | bytes 983048 | tf_op jit(solution)/shard_map/ppermute | solution.py:388
  33.4 11.7 %collective-permute-start.5 = (bf16[10,128,128]{2,1,0:T(8,128)(2,1)S(1)}, bf16[10,128,128]{2,1,0:T(8,128)(2,1)S(1)}, u32[]{:S(2)}, u32[]{:S(2)}) collective-permute-start(bf16[10,128,128]{2,1,0:T(8,128)(2,1)S(1)} %get-tuple-element.61), channel_id=1, source_target_pairs={{1,2},{2,1},{3,4},{4,3},{5,6},{6,5},{7,8},{8,7},{9,10},{10,9},{11,... | collective-permute-start | bytes 983048 | tf_op jit(solution)/shard_map/ppermute | solution.py:388
